TPU v7x, 32 devices: a whole 2x2x4 slice. The times are simulated.
32 devices in a mesh: tile: 4 (over x, core), tm: 8 (over z, y).
Axes of the slice: x: 2, y: 2, z: 4, core: 2. Of those that a mesh axis runs over, the one named last changes fastest.
Arguments:
- movie: bfloat16 [128, 256, 512], P('tile', None, 'tm'), may hold values from -6 to 6
- footprints: bfloat16 [32, 4, 32, 32, 128], P('tile'), may hold values from -0.5 to 0.5
- support: int32 [32, 4], P('tile'), may hold values from -1 to 31, as said below
- cycle_offsets: int32 [48, 2], replicated, may hold values from -8 to 8, as said below
- cycle_weights: float32 [48, 128, 256], P(None, 'tile'), may hold values from -0.875 to 0.875
- owner_map: int32 [32], replicated, may hold values from 0 to 31, each once
- traces_old: bfloat16 [4096, 512], P(('tile', 'tm')), may hold values from 0 to 2
- taps: float32 [129], replicated, may hold values from -0.5 to 0.5
Outputs:
- residual: bfloat16 [128, 256, 512], P('tile', None, 'tm')
- traces_new: bfloat16 [4096, 512], P(('tile', 'tm'))
Inputs may be any that keep to these rules, and one draw needn't show every extreme that they name: `support`: in every row the live slots come first and name distinct blocks; -1 marks the empty slots. Every tile has 1 to 4 live slots, and every tile row (the 8 tiles t with equal t // 8) has exactly 20 live slots in all. `cycle_offsets`: rows are distinct (row offset, column offset) pairs; each has max(|row offset|, |column offset|) between 6 and 8; one row offset is 8 and one is -8. `owner_map`: each block has its own position.
All inputs are finite; a program needn't handle non-finite values.
Results may differ from a plain program's by a relative error of at most 0.0075.
Values may be sent and summed in bfloat16 or wider, within the bound.
No kernel may reach another device: no remote copies, remote signals or barrier semaphores. Data moves between devices by JAX's collectives and lax.ppermute only.
A program may use at most 128 MiB of HBM per device.

v0:
```python
import jax
import jax.numpy as jnp
from jax import lax
from jax.sharding import PartitionSpec as P

TILE = 32
BLOCK = 128
NBLK = 32
RAD = 8
TBLK = 256


ridge_term = 1.0
highest = lax.Precision.HIGHEST


def padded_2(array, sides, width):
    for axis, dim in sides:
        peers, length = (lax.axis_size(axis), array.shape[dim])
        up = [(i, (i + 1) % peers) for i in range(peers - 1)]
        down = [(j, i) for i, j in up]
        last = lax.slice_in_dim(array, length - width, length, axis=dim)
        initial = lax.slice_in_dim(array, 0, width, axis=dim)
        before = lax.ppermute(last, axis, up)
        after = lax.ppermute(initial, axis, down)
        array = jnp.concatenate([before, array, after], axis=dim)
    return array


def cycle_sum(padded, weights, cycle_offsets, out_rows, col_count):
    frames = padded.shape[2]
    running = jnp.zeros((out_rows, col_count, frames), jnp.float32)
    for cycle_index in range(cycle_offsets.shape[0]):
        start_row = RAD + cycle_offsets[cycle_index, 0]
        start_col = RAD + cycle_offsets[cycle_index, 1]
        shifted = lax.dynamic_slice(
            padded, (start_row, start_col, jnp.zeros((), jnp.int32)), (out_rows, col_count, frames)
        )
        running = running + weights[cycle_index][:, :, None] * shifted.astype(jnp.float32)
    return running


def widen_cols(field_in):
    return jnp.pad(field_in, ((0, 0), (RAD, RAD), (0, 0)))


def clean_rows(field_in, weights, cycle_offsets):
    extended = padded_2(field_in, (("tile", 0),), RAD)
    backdrop = cycle_sum(
        widen_cols(extended), weights, cycle_offsets, field_in.shape[0], field_in.shape[1]
    )
    return (field_in.astype(jnp.float32) - backdrop).astype(jnp.bfloat16)


def to_tiles(owned):
    group_traces = lax.all_to_all(owned, "tm", split_axis=1, concat_axis=0, tiled=True)
    return lax.all_gather(group_traces, "tile", axis=0, tiled=True)


def neural_part(footprints, live_slot, position, traces_full, row_count, col_count):
    frame_count = traces_full.shape[1]
    blocks = traces_full.reshape(NBLK, BLOCK, frame_count)
    picked = jnp.take(blocks, jnp.maximum(position, 0), axis=0)
    picked = jnp.where(live_slot[:, :, None, None], picked, jnp.zeros((), jnp.bfloat16))
    neural_image = jnp.einsum(
        "tkrcn,tknf->rtcf", footprints, picked, preferred_element_type=jnp.float32
    )
    return neural_image.reshape(row_count, col_count, frame_count)


def band_tables(taps):
    half_taps = (taps.shape[0] - 1) // 2
    source_pos = jnp.arange(TBLK, dtype=jnp.int32)[:, None]
    target_pos = jnp.arange(TBLK, dtype=jnp.int32)[None, :]
    matrices = []
    for block_shift in (-1, 0, 1):
        tap_ids = target_pos - source_pos - block_shift * TBLK + half_taps
        inside = (tap_ids >= 0) & (tap_ids <= 2 * half_taps)
        matrices.append(jnp.where(inside, taps[jnp.clip(tap_ids, 0, 2 * half_taps)], 0.0))
    return matrices


def wiener_blocks(update, taps):
    owned_count, frames = update.shape
    block_total = frames // TBLK
    blocks = update.reshape(owned_count, block_total, TBLK)
    empty_block = jnp.zeros((owned_count, 1, TBLK), jnp.float32)
    before = jnp.concatenate([empty_block, blocks[:, :-1]], axis=1)
    after_blocks = jnp.concatenate([blocks[:, 1:], empty_block], axis=1)
    matrices = band_tables(taps)
    running = jnp.einsum("nbs,st->nbt", before, matrices[0], precision=highest)
    running = running + jnp.einsum("nbs,st->nbt", blocks, matrices[1], precision=highest)
    running = running + jnp.einsum("nbs,st->nbt", after_blocks, matrices[2], precision=highest)
    return running.reshape(owned_count, frames)


def body(movie, footprints, support, cycle_offsets, cycle_weights, owner_map, traces_old, taps):
    row_count, col_count, frames = movie.shape
    tile_count = lax.axis_size("tile")
    time_count = lax.axis_size("tm")
    owned_count = traces_old.shape[0]
    tiles_here, slot_count = support.shape
    live_slot = support >= 0
    block_ids = jnp.arange(NBLK, dtype=jnp.int32)
    matches = jnp.maximum(support, 0)[:, :, None] == block_ids
    position = jnp.sum(jnp.where(matches, owner_map, 0), axis=2)
    neural_old = neural_part(
        footprints, live_slot, position, to_tiles(traces_old), row_count, col_count
    )
    first_res = (movie.astype(jnp.float32) - neural_old).astype(jnp.bfloat16)
    second_res = clean_rows(first_res, cycle_weights, cycle_offsets)
    third_res = clean_rows(second_res, cycle_weights, cycle_offsets)
    tile_view = third_res.reshape(row_count, tiles_here, TILE, frames)
    slot_proj = jnp.einsum(
        "tkrcn,rtcf->tknf", footprints, tile_view, preferred_element_type=jnp.float32
    )
    selector = (
        (position.reshape(-1)[None, :] == block_ids[:, None]) & live_slot.reshape(-1)[None, :]
    ).astype(jnp.float32)
    partial_sums = jnp.einsum(
        "bs,snf->bnf",
        selector,
        slot_proj.reshape(tiles_here * slot_count, BLOCK, frames),
        precision=highest,
    ).reshape(NBLK * BLOCK, frames)
    footprint_f = footprints.astype(jnp.float32)
    squares = jnp.sum(footprint_f * footprint_f, axis=(2, 3)).reshape(
        tiles_here * slot_count, BLOCK
    )
    partial_norms = jnp.dot(selector, squares, precision=highest).reshape(NBLK * BLOCK)
    tile_here = lax.axis_index("tile")
    time_here = lax.axis_index("tm")
    delivered = lax.all_to_all(
        partial_sums, ("tile", "tm"), split_axis=0, concat_axis=1, tiled=True
    )
    owned_sums = jnp.sum(
        delivered.reshape(owned_count, tile_count, time_count, frames), axis=1
    ).reshape(owned_count, time_count * frames)
    total_norms = lax.psum(partial_norms, "tile")
    owned_norms = lax.dynamic_slice_in_dim(
        total_norms, (tile_here * time_count + time_here) * owned_count, owned_count
    )
    update = traces_old.astype(jnp.float32) + owned_sums / (owned_norms[:, None] + ridge_term)
    filtered = wiener_blocks(update, taps)
    fresh_traces = jnp.maximum(filtered, 0.0).astype(jnp.bfloat16)
    neural_new = neural_part(
        footprints, live_slot, position, to_tiles(fresh_traces), row_count, col_count
    )
    residual = (third_res.astype(jnp.float32) + neural_old - neural_new).astype(jnp.bfloat16)
    return (residual, fresh_traces)


def solution(mesh):
    return jax.shard_map(
        body,
        mesh=mesh,
        in_specs=(
            P("tile", None, "tm"),
            P("tile", None, None, None, None),
            P("tile", None),
            P(),
            P(None, "tile", None),
            P(),
            P(("tile", "tm"), None),
            P(),
        ),
        out_specs=(P("tile", None, "tm"), P(("tile", "tm"), None)),
        check_vma=False,
    )
```

profile of v0, /device:TPU:0, one launch (start us, length us, event | category | flops | bytes accessed | tf_op | source)
XLA Modules:
  0.0 1648.9 jit_solution(18138984720887346867)
XLA Ops:
  0.7 1.8 copy.112
  2.4 7.3 all-to-all-start
  9.7 0.7 broadcast_maximum_fusion.1
  10.4 0.9 select_reduce_fusion
  11.3 0.7 broadcast_compare_fusion
  12.0 1.3 slice.738
  13.2 2.1 fusion.88
  40.3 2.1 fusion.89
  66.4 2.1 fusion.86
  92.5 2.1 fusion.87
  117.5 2.1 fusion.90
  122.6 0.1 copy.157
  122.8 1.8 slice_bitcast_fusion.47
  124.7 1.8 copy.109
  126.5 1.7 slice_bitcast_fusion.45
  128.1 7.2 all_gather.6
  135.5 0.7 gather_fusion.3
  136.1 5.8 convolution_bitcast_fusion.1
  141.9 0.6 copy.117
  142.6 0.9 copy-done.7
  143.5 0.6 fusion.2
  144.1 1.5 fusion.85
  145.6 0.3 copy-done.1
  145.9 2.3 collective-permute-start
  148.2 1.3 collective-permute-start.1
  171.5 0.1 copy.156
  172.6 1.2 slice_bitcast_fusion.46
  174.0 2.5 select_maximum_fusion.2
  176.7 83.6 %subtract_convert_fusion.1 = bf16[32,256,64]{2,1,0:T(8,128)(2,1)S(1)} fusion(bf16[32,256,64]{2,1,0:T(8,128)(2,1)S(1)} %fusion.2, bf16[48,272,64]{2,1,0:T(8,128)(2,1)S(1)} %select_maximum_fusion.2, s32[]{:T(128)S(6)} %select_n.541, s32[]{:T(128)S(6)} %select_n.542, f32[32,256]{1,0:T(8,128)S(1)} %copy-done.64, s32[]{:T(128)S(6)} %select_n.539, ...), kind=kLoop, calls=%fused_computation.15 | loop fusion | flops 76546048 | bytes 54002048 | tf_op jit(solution)/shard_map/convert_element_type | solution.py:52
  260.5 1.3 copy-done.3
  261.8 1.1 fusion.84
  262.9 3.9 collective-permute-start.2
  266.8 1.5 collective-permute-start.3
  268.3 0.6 and.25
  269.0 0.6 eq.31
  269.7 408.0 %gather_fusion.2 = f32[65536]{0:T(1024)S(1)} fusion(f32[129]{0:T(256)S(1)} %copy-done, s32[65536]{0:T(1024)S(1)} %broadcast_clamp_fusion), kind=kCustom, calls=%fused_computation.4 | custom fusion | bytes 786432 | tf_op jit(solution)/shard_map/gather | solution.py:79
  677.7 0.8 reshape.619
  678.4 408.0 %gather_fusion.1 = f32[65536]{0:T(1024)S(1)} fusion(f32[129]{0:T(256)S(1)} %copy-done, s32[65536]{0:T(1024)S(1)} %broadcast_clamp_fusion.1), kind=kCustom, calls=%fused_computation.3 | custom fusion | bytes 786432 | tf_op jit(solution)/shard_map/gather | solution.py:79
  1086.9 0.1 copy.155
  1087.1 2.7 select_maximum_fusion
  1090.1 86.9 %subtract_convert_fusion = bf16[32,256,64]{2,1,0:T(8,128)(2,1)S(1)} fusion(bf16[32,256,64]{2,1,0:T(8,128)(2,1)S(1)} %copy-done.4, bf16[48,272,64]{2,1,0:T(8,128)(2,1)S(1)} %select_maximum_fusion, s32[]{:T(128)S(6)} %select_n.541, s32[]{:T(128)S(6)} %select_n.542, s32[]{:T(128)S(6)} %select_n.539, s32[]{:T(128)S(6)} %select_n.540, s32[]{:T(128)S(6)} %select_n.537, ...), kind=kLoop, calls=%fused_computation.14 | loop fusion | flops 76546048 | bytes 54002048 | tf_op jit(solution)/shard_map/convert_element_type | solution.py:52
  1177.1 1.6 fusion.4
  1178.7 1.3 fusion.8
  1180.0 1.6 copy.124
  1181.6 7.7 all-to-all-start.1
  1189.3 408.0 %gather_fusion = f32[65536]{0:T(1024)S(1)} fusion(f32[129]{0:T(256)S(1)} %copy-done, s32[65536]{0:T(1024)S(1)} %broadcast_clamp_fusion.2), kind=kCustom, calls=%fused_computation.2 | custom fusion | bytes 786432 | tf_op jit(solution)/shard_map/gather | solution.py:79
  1597.4 5.1 multiply_reduce_fusion
  1602.6 11.5 psum.7
  1614.3 1.0 fusion.23
  1615.2 0.6 fusion.21
  1615.8 0.4 convolution_add_fusion.1
  1616.2 0.4 fusion.7
  1616.7 0.8 copy.130
  1617.4 5.5 all-to-all-start.2
  1623.0 1.7 copy.138
  1624.7 5.6 all-to-all-done.2
  1630.3 6.5 all_gather.7
  1637.0 0.6 gather_fusion.4
  1637.7 5.8 convolution_bitcast_fusion
  1643.5 0.5 copy.135
  1644.0 1.7 copy-done.2
  1645.7 0.7 copy-done.6
  1646.3 0.9 fusion.1
  1647.3 1.6 copy.137
  (232 shorter events, 1.8 us)
Async XLA Ops:
  0.6 269.0 %copy-start = (f32[129]{0:T(256)S(1)}, f32[129]{0:T(256)}, u32[]{:S(2)}) copy-start(f32[129]{0:T(256)} %param.17) | copy-start | bytes 1552
  0.6 124.0 %copy-start.8 = (bf16[32,256,64]{1,2,0:T(8,128)(2,1)S(1)}, bf16[32,256,64]{1,2,0:T(8,128)(2,1)}, u32[]{:S(2)}) copy-start(bf16[32,256,64]{1,2,0:T(8,128)(2,1)} %param.10) | copy-start | bytes 3145732
  2.4 125.7 %all-to-all-start = ((bf16[128,8,64]{0,2,1:T(8,128)(2,1)}), bf16[128,8,64]{0,2,1:T(8,128)(2,1)S(1)}, u32[]{:S(2)}, u32[]{:S(2)}) async-start(bf16[128,8,64]{0,2,1:T(8,128)(2,1)} %bitcast), calls=%async_computation | async-start | bytes 262144 | tf_op jit(solution)/shard_map/all_to_all | solution.py:56
  122.3 13.8 copy-start.94
  122.4 145.9 %copy-start.96 = (pred[8,4]{1,0:T(8,128)(4,1)}, pred[8,4]{1,0:T(8,128)(4,1)S(1)}, u32[]{:S(2)}) copy-start(pred[8,4]{1,0:T(8,128)(4,1)S(1)} %copy.110) | copy-start | bytes 100
  122.6 13.5 copy-start.98
  124.7 51.8 %copy-start.10 = (f32[32,256]{1,0:T(8,128)}, f32[32,256]{1,0:T(8,128)S(1)}, u32[]{:S(2)}) copy-start(f32[32,256]{1,0:T(8,128)S(1)} %get-tuple-element.15) | copy-start | bytes 98308
  124.7 51.8 %copy-start.12 = (f32[32,256]{1,0:T(8,128)}, f32[32,256]{1,0:T(8,128)S(1)}, u32[]{:S(2)}) copy-start(f32[32,256]{1,0:T(8,128)S(1)} %get-tuple-element.16) | copy-start | bytes 98308
  124.7 51.8 %copy-start.14 = (f32[32,256]{1,0:T(8,128)}, f32[32,256]{1,0:T(8,128)S(1)}, u32[]{:S(2)}) copy-start(f32[32,256]{1,0:T(8,128)S(1)} %get-tuple-element.17) | copy-start | bytes 98308
  124.7 51.8 %copy-start.16 = (f32[32,256]{1,0:T(8,128)}, f32[32,256]{1,0:T(8,128)S(1)}, u32[]{:S(2)}) copy-start(f32[32,256]{1,0:T(8,128)S(1)} %get-tuple-element.18) | copy-start | bytes 98308
  145.9 28.0 %collective-permute-start = (bf16[8,256,64]{2,1,0:T(8,128)(2,1)}, bf16[8,256,64]{2,1,0:T(8,128)(2,1)S(1)}, u32[]{:S(2)}, u32[]{:S(2)}) collective-permute-start(bf16[8,256,64]{2,1,0:T(8,128)(2,1)} %get-tuple-element.13), channel_id=1, source_target_pairs={{0,8},{8,16},{16,24},{1,9},{9,17},{17,25},{2,10},{10,18},{18,26},{... | collective-permute-start | bytes 786440 | tf_op jit(solution)/shard_map/ppermute | solution.py:24
  148.2 25.8 %collective-permute-start.1 = (bf16[8,256,64]{2,1,0:T(8,128)(2,1)}, bf16[8,256,64]{2,1,0:T(8,128)(2,1)}, u32[]{:S(2)}, u32[]{:S(2)}) collective-permute-start(bf16[8,256,64]{2,1,0:T(8,128)(2,1)} %get-tuple-element.14), channel_id=1, source_target_pairs={{8,0},{16,8},{24,16},{9,1},{17,9},{25,17},{10,2},{18,10},{26,18},{... | collective-permute-start | bytes 786440 | tf_op jit(solution)/shard_map/ppermute | solution.py:25
  171.6 4.9 copy-start.18
  171.6 4.9 copy-start.20
  171.6 4.9 copy-start.22
  171.6 4.9 copy-start.24
  171.6 4.9 copy-start.26
  171.7 4.9 copy-start.28
  171.7 4.9 copy-start.30
  171.7 4.9 copy-start.32
  172.4 4.2 copy-start.34
  172.4 4.2 copy-start.36
  172.4 4.2 copy-start.38
  172.4 4.2 copy-start.40
  172.4 4.2 copy-start.42
  172.4 4.2 copy-start.44
  172.5 4.2 copy-start.46
  172.5 4.2 copy-start.48
  172.5 4.2 copy-start.50
  172.5 4.2 copy-start.52
  172.5 4.2 copy-start.54
  172.5 4.2 copy-start.56
  172.5 4.2 copy-start.58
  172.5 4.2 copy-start.60
  173.7 86.5 %copy-start.68 = (f32[32,256]{1,0:T(8,128)}, f32[32,256]{1,0:T(8,128)S(1)}, u32[]{:S(2)}) copy-start(f32[32,256]{1,0:T(8,128)S(1)} %get-tuple-element.34) | copy-start | bytes 98308
  173.8 86.5 %copy-start.70 = (f32[32,256]{1,0:T(8,128)}, f32[32,256]{1,0:T(8,128)S(1)}, u32[]{:S(2)}) copy-start(f32[32,256]{1,0:T(8,128)S(1)} %get-tuple-element.35) | copy-start | bytes 98308
  173.8 86.5 %copy-start.72 = (f32[32,256]{1,0:T(8,128)}, f32[32,256]{1,0:T(8,128)S(1)}, u32[]{:S(2)}) copy-start(f32[32,256]{1,0:T(8,128)S(1)} %get-tuple-element.36) | copy-start | bytes 98308
  173.8 86.5 %copy-start.74 = (f32[32,256]{1,0:T(8,128)}, f32[32,256]{1,0:T(8,128)S(1)}, u32[]{:S(2)}) copy-start(f32[32,256]{1,0:T(8,128)S(1)} %get-tuple-element.37) | copy-start | bytes 98308
  173.8 86.5 %copy-start.76 = (f32[32,256]{1,0:T(8,128)}, f32[32,256]{1,0:T(8,128)S(1)}, u32[]{:S(2)}) copy-start(f32[32,256]{1,0:T(8,128)S(1)} %get-tuple-element.38) | copy-start | bytes 98308
  173.8 86.5 %copy-start.78 = (f32[32,256]{1,0:T(8,128)}, f32[32,256]{1,0:T(8,128)S(1)}, u32[]{:S(2)}) copy-start(f32[32,256]{1,0:T(8,128)S(1)} %get-tuple-element.39) | copy-start | bytes 98308
  173.8 86.5 %copy-start.80 = (f32[32,256]{1,0:T(8,128)}, f32[32,256]{1,0:T(8,128)S(1)}, u32[]{:S(2)}) copy-start(f32[32,256]{1,0:T(8,128)S(1)} %get-tuple-element.40) | copy-start | bytes 98308
  173.8 86.5 %copy-start.82 = (f32[32,256]{1,0:T(8,128)}, f32[32,256]{1,0:T(8,128)S(1)}, u32[]{:S(2)}) copy-start(f32[32,256]{1,0:T(8,128)S(1)} %get-tuple-element.41) | copy-start | bytes 98308
  173.8 86.5 %copy-start.83 = (f32[32,256]{1,0:T(8,128)}, f32[32,256]{1,0:T(8,128)S(1)}, u32[]{:S(2)}) copy-start(f32[32,256]{1,0:T(8,128)S(1)} %get-tuple-element.42) | copy-start | bytes 98308
  173.8 86.5 %copy-start.84 = (f32[32,256]{1,0:T(8,128)}, f32[32,256]{1,0:T(8,128)S(1)}, u32[]{:S(2)}) copy-start(f32[32,256]{1,0:T(8,128)S(1)} %get-tuple-element.43) | copy-start | bytes 98308
  173.8 86.5 %copy-start.85 = (f32[32,256]{1,0:T(8,128)}, f32[32,256]{1,0:T(8,128)S(1)}, u32[]{:S(2)}) copy-start(f32[32,256]{1,0:T(8,128)S(1)} %get-tuple-element.44) | copy-start | bytes 98308
  173.9 86.5 %copy-start.86 = (f32[32,256]{1,0:T(8,128)}, f32[32,256]{1,0:T(8,128)S(1)}, u32[]{:S(2)}) copy-start(f32[32,256]{1,0:T(8,128)S(1)} %get-tuple-element.45) | copy-start | bytes 98308
  173.9 86.5 %copy-start.87 = (f32[32,256]{1,0:T(8,128)}, f32[32,256]{1,0:T(8,128)S(1)}, u32[]{:S(2)}) copy-start(f32[32,256]{1,0:T(8,128)S(1)} %get-tuple-element.46) | copy-start | bytes 98308
  173.9 86.5 %copy-start.88 = (f32[32,256]{1,0:T(8,128)}, f32[32,256]{1,0:T(8,128)S(1)}, u32[]{:S(2)}) copy-start(f32[32,256]{1,0:T(8,128)S(1)} %get-tuple-element.47) | copy-start | bytes 98308
  173.9 86.5 %copy-start.89 = (f32[32,256]{1,0:T(8,128)}, f32[32,256]{1,0:T(8,128)S(1)}, u32[]{:S(2)}) copy-start(f32[32,256]{1,0:T(8,128)S(1)} %get-tuple-element.48) | copy-start | bytes 98308
  173.9 86.5 %copy-start.90 = (f32[32,256]{1,0:T(8,128)}, f32[32,256]{1,0:T(8,128)S(1)}, u32[]{:S(2)}) copy-start(f32[32,256]{1,0:T(8,128)S(1)} %get-tuple-element.49) | copy-start | bytes 98308
  173.9 86.5 %copy-start.91 = (f32[32,256]{1,0:T(8,128)}, f32[32,256]{1,0:T(8,128)S(1)}, u32[]{:S(2)}) copy-start(f32[32,256]{1,0:T(8,128)S(1)} %get-tuple-element.50) | copy-start | bytes 98308
  173.9 86.5 %copy-start.92 = (f32[32,256]{1,0:T(8,128)}, f32[32,256]{1,0:T(8,128)S(1)}, u32[]{:S(2)}) copy-start(f32[32,256]{1,0:T(8,128)S(1)} %get-tuple-element.51) | copy-start | bytes 98308
  173.9 86.5 %copy-start.93 = (f32[32,256]{1,0:T(8,128)}, f32[32,256]{1,0:T(8,128)S(1)}, u32[]{:S(2)}) copy-start(f32[32,256]{1,0:T(8,128)S(1)} %get-tuple-element.52) | copy-start | bytes 98308
  262.9 824.2 %collective-permute-start.2 = (bf16[8,256,64]{2,1,0:T(8,128)(2,1)}, bf16[8,256,64]{2,1,0:T(8,128)(2,1)}, u32[]{:S(2)}, u32[]{:S(2)}) collective-permute-start(bf16[8,256,64]{2,1,0:T(8,128)(2,1)} %get-tuple-element.11), channel_id=1, source_target_pairs={{0,8},{8,16},{16,24},{1,9},{9,17},{17,25},{2,10},{10,18},{18,26},{... | collective-permute-start | bytes 786440 | tf_op jit(solution)/shard_map/ppermute | solution.py:24
  266.8 820.2 %collective-permute-start.3 = (bf16[8,256,64]{2,1,0:T(8,128)(2,1)}, bf16[8,256,64]{2,1,0:T(8,128)(2,1)}, u32[]{:S(2)}, u32[]{:S(2)}) collective-permute-start(bf16[8,256,64]{2,1,0:T(8,128)(2,1)} %get-tuple-element.12), channel_id=1, source_target_pairs={{8,0},{16,8},{24,16},{9,1},{17,9},{25,17},{10,2},{18,10},{26,18},{... | collective-permute-start | bytes 786440 | tf_op jit(solution)/shard_map/ppermute | solution.py:25
  678.4 408.6 %copy-start.4 = (bf16[32,256,64]{2,1,0:T(8,128)(2,1)S(1)}, bf16[32,256,64]{2,1,0:T(8,128)(2,1)}, u32[]{:S(2)}) copy-start(bf16[32,256,64]{2,1,0:T(8,128)(2,1)} %copy-done.3) | copy-start | bytes 3145732
  1087.0 90.0 %slice-start = ((s8[8388608]{0:T(1024)(128)(4,1)}), s8[4194304]{0:T(1024)(128)(4,1)S(1)}, s32[]{:S(2)}) async-start(s8[8388608]{0:T(1024)(128)(4,1)} %bitcast.409), calls=%async_computation.3 | async-start | bytes 8388608
  1090.1 87.0 %slice-start.1 = ((s8[8388608]{0:T(1024)(128)(4,1)}), s8[4194304]{0:T(1024)(128)(4,1)S(1)}, s32[]{:S(2)}) async-start(s8[8388608]{0:T(1024)(128)(4,1)} %bitcast.409), calls=%async_computation.4 | async-start | bytes 8388608
  1181.6 432.6 %all-to-all-start.1 = ((f32[32,128,64]{1,2,0:T(8,128)}), f32[32,128,64]{1,2,0:T(8,128)S(1)}, u32[]{:S(2)}, u32[]{:S(2)}) async-start(f32[32,128,64]{1,2,0:T(8,128)} %copy.124), calls=%async_computation.1 | async-start | bytes 2097152 | tf_op jit(solution)/shard_map/all_to_all | solution.py:133
  1597.4 18.9 %copy-start.9 = (f32[256,256]{1,0:T(8,128)S(1)}, f32[256,256]{1,0:T(8,128)}, u32[]{:S(2)}) copy-start(f32[256,256]{1,0:T(8,128)} %reshape.619) | copy-start | bytes 786436
  1602.5 34.5 %copy-start.99 = (s32[1024]{0:T(1024)S(1)}, s32[1024]{0:T(1024)}, u32[]{:S(2)}) copy-start(s32[1024]{0:T(1024)} %copy-done.98) | copy-start | bytes 12292
  1614.2 23.4 %copy-start.95 = (pred[8,4]{1,0:T(8,128)(4,1)S(1)}, pred[8,4]{1,0:T(8,128)(4,1)}, u32[]{:S(2)}) copy-start(pred[8,4]{1,0:T(8,128)(4,1)} %copy-done.94) | copy-start | bytes 100
  1614.2 23.4 %copy-start.97 = (pred[8,4]{1,0:T(8,128)(4,1)S(1)}, pred[8,4]{1,0:T(8,128)(4,1)}, u32[]{:S(2)}) copy-start(pred[8,4]{1,0:T(8,128)(4,1)} %copy-done.96) | copy-start | bytes 100
  1617.4 12.9 all-to-all-start.2
  (47 other events, 146.7 us)
where the time goes:
time: 1650 us
  local copies, waits for them, and re-layouts  1260 us (76%)
  other arithmetic  186 us (11%)
  between operations  124 us (8%)
  starting transfers between devices  29.5 us (2%)
  blocking collectives  25.2 us (2%)
    gather x6, local copies, waits for them, and re-layouts, band_tables(): taps[jnp.clip(tap_ids, 0, 2 * half_taps)]  1220 us
    convert_element_type x2, other arithmetic, clean_rows(): return (field_in.astype(jnp.float32) - backdrop).astype(jnp.bfloat16)  170 us
  transfers between devices with their start and end apart: 7, of which 1 were waited for; matrix products, arithmetic and copies ran while one was open for 76% of the time, Pallas kernels for 0%

commit v1 on v0

v1 whole, which is shorter than its diff:
```python
import functools

import jax
import jax.numpy as jnp
from jax import lax
from jax.experimental import pallas as pl
from jax.experimental.pallas import tpu as pltpu
from jax.sharding import PartitionSpec as P

RAD = 8
LANES = 128
ROW_STEP = 8
AHEAD = 4
FIRST_VMEM = 53
FINAL_VMEM = 53
TAP_GROUP = 4
MIB = 1024 * 1024
FRAME_PARTS = 2
ridge_term = 1.0
highest = lax.Precision.HIGHEST
bf16 = jnp.bfloat16
f32 = jnp.float32
NT = (((1,), (1,)), ((), ()))
NN = (((1,), (0,)), ((), ()))

smem = pl.BlockSpec(memory_space=pltpu.SMEM)
vmem = pl.BlockSpec(memory_space=pltpu.VMEM)
anywhere = pl.BlockSpec(memory_space=pl.ANY)


def swap_groups(parts, width):
    count = len(parts)
    lane = lax.broadcasted_iota(jnp.int32, parts[0].shape, 1)
    dist = count // 2
    while dist >= 1:
        upper = (lane // (width * dist)) % 2 == 1
        out = list(parts)
        for a in range(count):
            if a & dist:
                continue
            low, high = parts[a], parts[a | dist]
            out[a] = jnp.where(upper, pltpu.roll(high, width * dist, 1), low)
            out[a | dist] = jnp.where(upper, high, pltpu.roll(low, LANES - width * dist, 1))
        parts = out
        dist //= 2
    return parts


def slot_position(support_ref, owner_ref, slot):
    slots = support_ref.shape[0]
    block = support_ref[slot % slots, slot // slots]
    return jnp.where(block >= 0, owner_ref[jnp.maximum(block, 0)], -1)


def place_of(position, here, tile_count, share):
    apart = (position // share) ^ here
    bits = tile_count.bit_length() - 1
    rank = sum(((apart >> b) & 1) << (bits - 1 - b) for b in range(bits))
    return rank * share + position % share


def gather_lhs(support_ref, owner_ref, here_ref, pieces, lhs_ref):
    tile_count = len(pieces[0])
    share = pieces[0][0].shape[0]
    for slot in range(2 * lhs_ref.shape[0]):
        position = slot_position(support_ref, owner_ref, slot)
        live = position >= 0
        index = jnp.maximum(position, 0)
        apart = (index // share) ^ here_ref[0]
        row = index % share
        parts = []
        for refs in pieces:
            value = refs[0][row]
            for rank in range(1, tile_count):
                value = jnp.where(apart == rank, refs[rank][row], value)
            parts.append(jnp.where(live, value, jnp.zeros_like(value)))
        value = parts[0] if len(parts) == 1 else jnp.concatenate(parts, axis=0)
        block = value.shape[1]
        lhs_ref[slot // 2, :, (slot % 2) * block : (slot % 2 + 1) * block] = value


def neural_rows(lhs_ref, chunk_ref):
    tiles, slots = chunk_ref.shape[:2]
    images = []
    for t in range(tiles):
        image = None
        for k in range(0, slots, 2):
            rhs = jnp.concatenate([chunk_ref[t, k + i] for i in range(2)], axis=1)
            part = lax.dot_general(
                lhs_ref[(t * slots + k) // 2], rhs, NT, preferred_element_type=f32
            )
            image = part if image is None else image + part
        images.append(image)
    return images


class Copies:
    def __init__(self, parts):
        self.parts = parts

    def start(self):
        for part in self.parts:
            part.start()

    def wait(self):
        for part in self.parts:
            part.wait()


def chunk_copies(tile, prints_ref, chunks_ref, sems):
    size = ROW_STEP * tile
    return [
        Copies(
            [
                pltpu.make_async_copy(
                    prints_ref.at[t, :, pl.ds(c * size, size), :], chunks_ref.at[c, t], sems.at[c, t]
                )
                for t in range(chunks_ref.shape[1])
            ]
        )
        for c in range(chunks_ref.shape[0])
    ]


def field_copies(field_ref, chunks_ref, sems):
    return [
        pltpu.make_async_copy(
            field_ref.at[pl.ds(c * ROW_STEP, ROW_STEP)], chunks_ref.at[c], sems.at[c]
        )
        for c in range(chunks_ref.shape[0])
    ]


def image_rows(tile, images, finish):
    group = LANES // tile
    for h in range(ROW_STEP // group):
        sides = []
        for g in range(0, len(images), group):
            cut = [im[:, h * LANES : (h + 1) * LANES] for im in images[g : g + group]]
            sides.append(swap_groups(cut, tile))
        for r in range(group):
            finish(h * group + r, jnp.concatenate([side[r] for side in sides], axis=1))


def write_edges(odd, first_rows, last_rows, inner_ref, outer_ref):
    @pl.when(odd == 1)
    def _():
        inner_ref[...] = last_rows()
        outer_ref[...] = first_rows()

    @pl.when(odd != 1)
    def _():
        inner_ref[...] = first_rows()
        outer_ref[...] = last_rows()


def first_kernel(tile, tile_count, support_ref, owner_ref, here_ref, split_ref, movie_ref, prints_ref, *refs):
    pieces = refs[:tile_count]
    out_ref, inner_ref, outer_ref, prints_buf, movie_buf, lhs_ref, prints_sem, movie_sem = refs[tile_count:]
    copies = chunk_copies(tile, prints_ref, prints_buf, prints_sem)
    movies = field_copies(movie_ref, movie_buf, movie_sem)
    for c in range(AHEAD):
        movies[c].start()
        copies[c].start()
    gather_lhs(support_ref, owner_ref, here_ref, (pieces,), lhs_ref)
    for c in range(len(copies)):
        movies[c].wait()
        copies[c].wait()
        if c + AHEAD < len(copies):
            movies[c + AHEAD].start()
            copies[c + AHEAD].start()
        images = neural_rows(lhs_ref, prints_buf.at[c])

        def finish(row, image):
            value = (movie_buf[c, row].astype(f32) - image).astype(bf16)
            moved = lax.dot_general(value, split_ref[...], NN, preferred_element_type=f32)
            out_ref[c * ROW_STEP + row] = moved.astype(bf16)

        image_rows(tile, images, finish)
    rows = out_ref.shape[0]
    write_edges(
        here_ref[0] % 2,
        lambda: out_ref[:RAD],
        lambda: out_ref[rows - RAD :],
        inner_ref,
        outer_ref,
    )


def edge_shapes(field):
    return [jax.ShapeDtypeStruct((RAD,) + field.shape[1:], bf16)] * 2


def first_call(support, owner, here, split, field, footprints, pieces):
    rows, frames, cols = field.shape
    tiles, slots, pixels, block = footprints.shape
    tile = cols // tiles
    chunks = rows // ROW_STEP
    return pl.pallas_call(
        functools.partial(first_kernel, tile, len(pieces)),
        name="first",
        in_specs=[smem, smem, smem, vmem, anywhere, anywhere] + [vmem] * len(pieces),
        out_specs=[vmem] * 3,
        out_shape=[jax.ShapeDtypeStruct(field.shape, bf16)] + edge_shapes(field),
        scratch_shapes=[
            pltpu.VMEM((chunks, tiles, slots, ROW_STEP * tile, block), bf16),
            pltpu.VMEM((chunks, ROW_STEP, frames, cols), bf16),
            pltpu.VMEM((tiles * slots // 2, frames, 2 * block), bf16),
            pltpu.SemaphoreType.DMA((chunks, tiles)),
            pltpu.SemaphoreType.DMA((chunks,)),
        ],
        compiler_params=pltpu.CompilerParams(vmem_limit_bytes=FIRST_VMEM * MIB),
    )(support, owner, here, split, field, footprints, *pieces)


def final_kernel(tile, tile_count, support_ref, owner_ref, here_ref, third_ref, prints_ref, *refs):
    old, new = refs[:tile_count], refs[tile_count : 2 * tile_count]
    out_ref, prints_buf, out_buf, lhs_ref, prints_sem, out_sem = refs[2 * tile_count :]
    frames = third_ref.shape[1]
    copies = chunk_copies(tile, prints_ref, prints_buf, prints_sem)
    results = [
        pltpu.make_async_copy(
            out_buf.at[c], out_ref.at[pl.ds(c * ROW_STEP, ROW_STEP)], out_sem.at[c]
        )
        for c in range(len(copies))
    ]
    for c in range(AHEAD):
        copies[c].start()
    gather_lhs(support_ref, owner_ref, here_ref, (old, new), lhs_ref)
    for c in range(len(copies)):
        copies[c].wait()
        if c + AHEAD < len(copies):
            copies[c + AHEAD].start()
        images = neural_rows(lhs_ref, prints_buf.at[c])
        images = [im[:frames] - im[frames:] for im in images]

        def finish(row, image):
            value = third_ref[c * ROW_STEP + row].astype(f32) + image
            out_buf[c, row] = value.astype(bf16)

        image_rows(tile, images, finish)
        results[c].start()
    for r in results:
        r.wait()


def final_call(support, owner, here, third, footprints, old, new):
    rows, frames, cols = third.shape
    tiles, slots, pixels, block = footprints.shape
    tile = cols // tiles
    chunks = rows // ROW_STEP
    return pl.pallas_call(
        functools.partial(final_kernel, tile, len(old)),
        name="final",
        in_specs=[smem, smem, smem, vmem, anywhere] + [vmem] * (2 * len(old)),
        out_specs=anywhere,
        out_shape=jax.ShapeDtypeStruct(third.shape, bf16),
        scratch_shapes=[
            pltpu.VMEM((chunks, tiles, slots, ROW_STEP * tile, block), bf16),
            pltpu.VMEM((chunks, ROW_STEP, frames, cols), bf16),
            pltpu.VMEM((tiles * slots // 2, 2 * frames, 2 * block), bf16),
            pltpu.SemaphoreType.DMA((chunks, tiles)),
            pltpu.SemaphoreType.DMA((chunks,)),
        ],
        compiler_params=pltpu.CompilerParams(vmem_limit_bytes=FINAL_VMEM * MIB),
    )(support, owner, here, third, footprints, *old, *new)


def tree_sum(terms):
    while len(terms) > 1:
        pairs = [a + b for a, b in zip(terms[::2], terms[1::2])]
        terms = pairs + terms[len(terms) - len(terms) % 2 :]
    return terms[0]


def cycle_pass(
    offsets_ref, here_ref, starts_ref, inner_ref, outer_ref, field_ref, weights_ref, out_ref,
    moved_ref, ready,
):
    rows, frames, cols = field_ref.shape
    extended = rows + 2 * RAD
    taps = weights_ref.shape[0]
    odd = here_ref[0] % 2 == 1
    width = cols // 2

    for j in range(taps):
        starts_ref[j] = (offsets_ref[1, j] + RAD) * extended + offsets_ref[0, j] + RAD
    sublanes = weights_ref.shape[2]
    shifts = range(-RAD, RAD + 1)

    def place_row(value, row, shifts, cache):
        sides = (value[:, :width], value[:, width:])

        def turned(p, m):
            if (p, m) not in cache:
                cache[p, m] = sides[p] if m == 0 else pltpu.roll(sides[p], (-m) % width, 1)
            return cache[p, m]

        for d in shifts:
            ends = [turned((p + d) % 2, (p + d) // 2) for p in range(2)]
            moved_ref[(d + RAD) * extended + row] = jnp.concatenate(ends, axis=1)

    def above(r):
        return jnp.where(odd, outer_ref[r], inner_ref[r])

    def below(r):
        return jnp.where(odd, inner_ref[r], outer_ref[r])

    def fill(source, count, base):
        def step(r, carry):
            place_row(source(r), base + r, shifts, {})
            return carry

        lax.fori_loop(0, count, step, 0)

    fill(lambda r: field_ref[r], RAD + 1, RAD)
    fill(above, RAD, 0)
    ready()
    groups = -(-taps // TAP_GROUP)
    span = frames // FRAME_PARTS
    parts = groups * FRAME_PARTS

    def sweep(first, count, source):
        def row_step(i, carry):
            y = first + i
            cache = {}
            value = None if source is None else source(i)
            for f in range(FRAME_PARTS):
                cut = slice(f * span, (f + 1) * span)
                total = jnp.zeros((span, cols), f32)
                for g in range(groups):
                    terms = []
                    for j in range(g * TAP_GROUP, min((g + 1) * TAP_GROUP, taps)):
                        weight = jnp.concatenate([weights_ref[j, y]] * (span // sublanes), axis=0)
                        terms.append(moved_ref[starts_ref[j] + y, cut, :] * weight)
                    total = total + tree_sum(terms).astype(f32)
                    if source is not None:
                        at = f * groups + g
                        part = shifts[at * len(shifts) // parts : (at + 1) * len(shifts) // parts]
                        place_row(value, y + 2 * RAD + 1, part, cache)
                out_ref[y, cut, :] = (field_ref[y, cut, :].astype(f32) - total).astype(bf16)
            return carry

        lax.fori_loop(0, count, row_step, 0)

    sweep(0, rows - RAD - 1, lambda i: field_ref[i + RAD + 1])
    sweep(rows - RAD - 1, RAD, below)
    sweep(rows - 1, 1, None)


def cycle_kernel(
    offsets_ref, here_ref, inner_ref, outer_ref, field_ref, weights_ref, out_ref, inner_out, outer_out,
    starts_ref, moved_ref, weights_buf, weights_sem,
):
    copy = pltpu.make_async_copy(weights_ref, weights_buf, weights_sem)
    copy.start()
    cycle_pass(
        offsets_ref, here_ref, starts_ref, inner_ref, outer_ref, field_ref, weights_buf, out_ref,
        moved_ref, copy.wait,
    )
    rows = out_ref.shape[0]
    write_edges(
        here_ref[0] % 2,
        lambda: out_ref[:RAD],
        lambda: out_ref[rows - RAD :],
        inner_out,
        outer_out,
    )


def cycle_call(offsets, here, inner, outer, field, weights):
    rows, frames, cols = field.shape
    banks = 2 * RAD + 1
    return pl.pallas_call(
        cycle_kernel,
        name="cycle",
        in_specs=[smem, smem, vmem, vmem, vmem, anywhere],
        out_specs=[vmem] * 3,
        out_shape=[jax.ShapeDtypeStruct(field.shape, bf16)] + edge_shapes(field),
        scratch_shapes=[
            pltpu.SMEM((weights.shape[0],), jnp.int32),
            pltpu.VMEM((banks * (rows + 2 * RAD), frames, cols), bf16),
            pltpu.VMEM(weights.shape, bf16),
            pltpu.SemaphoreType.DMA,
        ],
        compiler_params=pltpu.CompilerParams(vmem_limit_bytes=40 * MIB),
    )(offsets, here, inner, outer, field, weights)


def halo_rows(inner, outer):
    peers = lax.axis_size("tile")
    crossing = [(i, i + 1) for i in range(1, peers - 1, 2)]
    within = [(i, i + 1) for i in range(0, peers - 1, 2)]
    both = [pairs + [(j, i) for i, j in pairs] for pairs in (crossing, within)]
    return lax.ppermute(inner, "tile", both[0]), lax.ppermute(outer, "tile", both[1])


def square_sum(values):
    pixels, block = values.shape
    cut = values.reshape(pixels // LANES, LANES, block)
    return jnp.sum(
        tree_sum([cut[i] * cut[i] for i in range(pixels // LANES)]).astype(f32),
        axis=0,
        keepdims=True,
    )


def norm_kernel(
    share, tile_count, support_ref, owner_ref, here_ref, prints_ref, keep_ref, send_ref,
    buf_ref, sem_ref, square_ref,
):
    tiles, slots, pixels, block = prints_ref.shape
    half = keep_ref.shape[0]
    positions = 2 * half
    copies = [
        pltpu.make_async_copy(prints_ref.at[t], buf_ref.at[t], sem_ref.at[t]) for t in range(tiles)
    ]
    for c in copies:
        c.start()
    square_ref[...] = jnp.zeros_like(square_ref)
    for t in range(tiles):
        copies[t].wait()
        for k in range(0, slots, 2):
            pair = jnp.concatenate([buf_ref[t, k + i] for i in range(2)], axis=1)
            sums = square_sum(pair)
            for i in range(2):
                position = slot_position(support_ref, owner_ref, t * slots + k + i)
                place = place_of(jnp.maximum(position, 0), here_ref[0], tile_count, share)
                place = jnp.where(position >= 0, place, positions)
                square_ref[pl.ds(place, 1), :] += sums[:, i * block : (i + 1) * block]
    keep_ref[...] = square_ref[:half]
    squares = square_ref[half:positions]
    high = squares.astype(bf16)
    send_ref[:half] = high
    send_ref[half:] = (squares - high.astype(f32)).astype(bf16)


def norm_call(support, owner, here, footprints, tile_count):
    tiles, slots, pixels, block = footprints.shape
    positions = owner.shape[0]
    half = positions // 2
    return pl.pallas_call(
        functools.partial(norm_kernel, positions // tile_count, tile_count),
        name="norms",
        in_specs=[smem, smem, smem, anywhere],
        out_specs=[vmem] * 2,
        out_shape=[
            jax.ShapeDtypeStruct((half, block), f32),
            jax.ShapeDtypeStruct((2 * half, block), bf16),
        ],
        scratch_shapes=[
            pltpu.VMEM(footprints.shape, bf16),
            pltpu.SemaphoreType.DMA((tiles,)),
            pltpu.VMEM((positions + 8, block), f32),
        ],
        compiler_params=pltpu.CompilerParams(vmem_limit_bytes=FIRST_VMEM * MIB),
    )(support, owner, here, footprints)


def project_kernel(
    tile, tile_count, support_ref, owner_ref, offsets_ref, here_ref, join_ref, inner_ref, outer_ref,
    field_ref, norms_ref, weights_ref, prints_ref, whole_ref, keep_ref, send_ref,
    starts_ref, moved_ref, weights_buf, weights_sem, prints_buf, prints_sem, third_ref, lhs_ref, sum_ref,
):
    rows, frames, cols = field_ref.shape
    tiles, slots, pixels, block = prints_ref.shape
    group = LANES // tile
    half = keep_ref.shape[0]
    weights_copy = pltpu.make_async_copy(weights_ref, weights_buf, weights_sem)
    weights_copy.start()
    copies = [
        pltpu.make_async_copy(prints_ref.at[t], prints_buf.at[t], prints_sem.at[t])
        for t in range(tiles)
    ]
    for c in copies:
        c.start()
    sum_ref[...] = jnp.zeros_like(sum_ref)
    cycle_pass(
        offsets_ref, here_ref, starts_ref, inner_ref, outer_ref, field_ref, weights_buf, third_ref,
        moved_ref, weights_copy.wait,
    )
    positions = sum_ref.shape[0] - 1
    for h in range(rows // group):
        whole = []
        for r in range(group):
            row = h * group + r
            value = lax.dot_general(
                third_ref[row], join_ref[...], NN, preferred_element_type=f32
            )
            whole.append(value.astype(bf16))
            whole_ref[row] = whole[-1]
        for g in range(cols // LANES):
            cut = [w[:, g * LANES : (g + 1) * LANES] for w in whole]
            for t, part in enumerate(swap_groups(cut, tile)):
                lhs_ref[g * group + t, :, h * LANES : (h + 1) * LANES] = part
    for t in range(tiles):
        copies[t].wait()
        lhs = lhs_ref[t]
        for k in range(0, slots, 2):
            rhs = jnp.concatenate([prints_buf[t, k + i] for i in range(2)], axis=1)
            out = lax.dot_general(lhs, rhs, NN, preferred_element_type=f32)
            for i in range(2):
                position = slot_position(support_ref, owner_ref, t * slots + k + i)
                place = place_of(
                    jnp.maximum(position, 0), here_ref[0], tile_count, positions // tile_count
                )
                place = jnp.where(position >= 0, place, positions)
                sum_ref[place] += out[:, i * block : (i + 1) * block]
    keep_ref[...] = sum_ref[:half]
    send_ref[: half * frames] = sum_ref[half : 2 * half].reshape(half * frames, block).astype(bf16)
    send_ref[half * frames :] = norms_ref[...]


def project_call(
    support, owner, offsets, here, join, inner, outer, field, norms, weights, footprints, tile_count
):
    rows, frames, cols = field.shape
    tiles, slots, pixels, block = footprints.shape
    tile = cols // tiles
    positions = owner.shape[0]
    half = positions // 2
    banks = 2 * RAD + 1
    return pl.pallas_call(
        functools.partial(project_kernel, tile, tile_count),
        name="project",
        in_specs=[smem, smem, smem, smem, vmem, vmem, vmem, vmem, vmem, anywhere, anywhere],
        out_specs=[vmem] * 3,
        out_shape=[
            jax.ShapeDtypeStruct(field.shape, bf16),
            jax.ShapeDtypeStruct((half, frames, block), f32),
            jax.ShapeDtypeStruct((half * (frames + 2), block), bf16),
        ],
        scratch_shapes=[
            pltpu.SMEM((weights.shape[0],), jnp.int32),
            pltpu.VMEM((banks * (rows + 2 * RAD), frames, cols), bf16),
            pltpu.VMEM(weights.shape, bf16),
            pltpu.SemaphoreType.DMA,
            pltpu.VMEM(footprints.shape, bf16),
            pltpu.SemaphoreType.DMA((tiles,)),
            pltpu.VMEM(field.shape, bf16),
            pltpu.VMEM((tiles, frames, pixels), bf16),
            pltpu.VMEM((positions + 1, frames, block), f32),
        ],
        compiler_params=pltpu.CompilerParams(vmem_limit_bytes=52 * MIB),
    )(support, owner, offsets, here, join, inner, outer, field, norms, weights, footprints)


def gathered(value):
    peers = lax.axis_size("tile")
    pieces = {0: value}
    step = peers // 2
    while step >= 1:
        pairs = [(i, i ^ step) for i in range(peers)]
        for apart in sorted(pieces):
            pieces[apart ^ step] = lax.ppermute(pieces[apart], "tile", pairs)
        step //= 2
    return [pieces[apart] for apart in range(peers)]


def reduced(keep, norms, send):
    peers = lax.axis_size("tile")
    step = 1
    while True:
        half, frames, block = keep.shape
        arrived = lax.ppermute(send, "tile", [(i, i ^ step) for i in range(peers)]).astype(f32)
        keep = keep + arrived[: half * frames].reshape(keep.shape)
        norms = norms + arrived[half * frames : -half] + arrived[-half:]
        step *= 2
        if step == peers:
            return keep, norms
        half = half // 2
        high = norms[half:].astype(bf16)
        low = (norms[half:] - high.astype(f32)).astype(bf16)
        send = jnp.concatenate([keep[half:].astype(bf16).reshape(half * frames, block), high, low])
        keep, norms = keep[:half], norms[:half]


def filter_kernel(odd_ref, taps_ref, own_ref, even_ref, other_ref, out_ref):
    count, frames, block = own_ref.shape
    width = taps_ref.shape[1]
    base = jnp.broadcast_to(taps_ref[...], (frames, width))
    band = pltpu.roll(base, 0, 1, stride=1, stride_axis=0)
    before, here, after = (band[:, i * frames : (i + 1) * frames] for i in range(3))
    odd = odd_ref[0] == 1
    first = jnp.where(odd, before, after)
    second = jnp.where(odd, after, before)
    for q in range(count):
        out = lax.dot_general(here, own_ref[q], NN, precision=highest, preferred_element_type=f32)
        out += lax.dot_general(
            first, even_ref[q].astype(f32), NN, precision=highest, preferred_element_type=f32
        )
        out += lax.dot_general(
            second, other_ref[q].astype(f32), NN, precision=highest, preferred_element_type=f32
        )
        out_ref[q] = jnp.maximum(out, 0.0).astype(bf16)


def filter_call(odd, taps, own, even, other):
    frames = own.shape[1]
    reach = taps.shape[0]
    half = (reach - 1) // 2
    width = 4 * frames
    lead = frames - half
    line = jnp.pad(taps[::-1], (lead, width - reach - lead)).reshape(1, width)
    return pl.pallas_call(
        filter_kernel,
        name="wiener",
        in_specs=[smem, vmem, vmem, vmem, vmem],
        out_specs=vmem,
        out_shape=jax.ShapeDtypeStruct(own.shape, bf16),
        compiler_params=pltpu.CompilerParams(vmem_limit_bytes=16 * MIB),
    )(odd, line, own, even, other)


def body(movie, footprints, support, cycle_offsets, cycle_weights, owner_map, traces_old, taps):
    tile_count, time_count = lax.axis_size("tile"), lax.axis_size("tm")
    tile_here, time_here = lax.axis_index("tile"), lax.axis_index("tm")
    rows, cols, frames = movie.shape
    tiles, slots, tile, _, block = footprints.shape
    positions = owner_map.shape[0]
    share = positions // tile_count
    owned = traces_old.shape[0]
    prints = footprints.reshape(tiles, slots, tile * tile, block)

    field = movie.transpose(0, 2, 1)
    columns = jnp.arange(cols, dtype=jnp.int32)
    source = 2 * (columns % (cols // 2)) + columns // (cols // 2)
    split = (columns[:, None] == source[None, :]).astype(bf16)
    join = (source[:, None] == columns[None, :]).astype(bf16)
    reached = columns[None, :] + cycle_offsets[:, 1:2]
    inside = (reached >= 0) & (reached < cols)
    weights = jnp.where(inside[:, None, :], cycle_weights, 0.0).astype(bf16)
    weights = lax.dot_general(
        weights, split, (((2,), (0,)), ((), ())), preferred_element_type=f32
    ).astype(bf16)
    offsets, slots_held = cycle_offsets.T, support.T
    here = tile_here.astype(jnp.int32).reshape(1)

    outgoing = traces_old.T.reshape(time_count, frames, owned)
    group_old = lax.all_to_all(outgoing, "tm", split_axis=0, concat_axis=0, tiled=True)
    pieces = block // owned
    group_old = group_old.reshape(share, pieces, frames, owned).transpose(0, 2, 1, 3)
    group_old = group_old.reshape(share, frames, block)
    group_old, weights = lax.optimization_barrier((group_old, weights))
    old = gathered(group_old)

    first_res, inner, outer = first_call(slots_held, owner_map, here, split, field, prints, old)
    inner, weights = lax.optimization_barrier((inner, weights))
    inner, outer = halo_rows(inner, outer)
    weights = jnp.broadcast_to(weights[:, :, None, :], weights.shape[:2] + (8, cols))
    inner, outer, weights = lax.optimization_barrier((inner, outer, weights))
    second_res, inner, outer = cycle_call(offsets, here, inner, outer, first_res, weights)
    inner, tied = lax.optimization_barrier((inner, prints))
    inner, outer = halo_rows(inner, outer)
    norms, norms_away = norm_call(slots_held, owner_map, here, tied, tile_count)
    inner, outer, norms_away = lax.optimization_barrier((inner, outer, norms_away))
    third_res, keep, send = project_call(
        slots_held, owner_map, offsets, here, join, inner, outer, second_res, norms_away, weights,
        prints, tile_count,
    )
    total, norms = reduced(keep, norms, send)

    update = group_old.astype(f32) + total / (norms[:, None, :] + ridge_term)
    narrow = update.astype(bf16)
    even_pairs = [(i, i ^ 1) for i in range(time_count)]
    odd_pairs = [(i, i + 1) for i in range(1, time_count - 1, 2)]
    odd_pairs = odd_pairs + [(j, i) for i, j in odd_pairs]
    even = lax.ppermute(narrow, "tm", even_pairs)
    other = lax.ppermute(narrow, "tm", odd_pairs)
    parity = (time_here % 2).astype(jnp.int32).reshape(1)
    fresh = filter_call(parity, taps, update, even, other)

    new = gathered(fresh)
    leaving = fresh.reshape(share, frames, pieces, owned).transpose(0, 2, 1, 3)
    leaving = leaving.reshape(time_count, frames, owned)
    owner_new = lax.all_to_all(leaving, "tm", split_axis=0, concat_axis=0, tiled=True)
    residual = final_call(slots_held, owner_map, here, third_res, prints, old, new)
    residual, owner_new = lax.optimization_barrier((residual, owner_new))
    traces_new = owner_new.reshape(time_count * frames, owned).T
    return residual.transpose(0, 2, 1), traces_new


def solution(mesh):
    return jax.shard_map(
        body,
        mesh=mesh,
        in_specs=(
            P("tile", None, "tm"),
            P("tile", None, None, None, None),
            P("tile", None),
            P(),
            P(None, "tile", None),
            P(),
            P(("tile", "tm"), None),
            P(),
        ),
        out_specs=(P("tile", None, "tm"), P(("tile", "tm"), None)),
        check_vma=False,
    )
```

time: 1650 us -> 115 us (0.07)
  local copies, waits for them, and re-layouts: 1260 us -> 5.3 us
  other arithmetic: 186 us -> 0.4 us
  between operations: 124 us -> 0.94 us
  Pallas kernels: 0 us -> 53.8 us
  blocking collectives: 25.2 us -> 0 us
  waiting for transfers between devices: 5.66 us -> 22.2 us
    gather x8 -> x0, local copies, waits for them, and re-layouts: 1230 us -> none  [the longest x6 1220 us: band_tables(): taps[jnp.clip(tap_ids, 0, 2 * half_taps)]]
    convert_element_type x4 -> x5, other arithmetic: 172 us -> 0.23 us  [the longest x1 0.1 us: body(): split = (columns[:, None] == source[None, :]).astype(bf16)]
    pallas_call x0 -> x6, Pallas kernels: none -> 53.8 us  [the longest x1 18.6 us: project_call(): pl.pallas_call(functools.partial(project_kernel, tile, tile_count), name=...]
    ppermute x4 -> x14, waiting for transfers between devices: 0.01 us -> 17.4 us  [the longest x6 5.94 us: gathered(): pieces[apart ^ step] = lax.ppermute(pieces[apart], 'tile', pairs)]
  transfers between devices with their start and end apart: 7 -> 16, of which waited for: 1 -> 9; matrix products, arithmetic and copies ran while one was open for 76% -> 2% of each run, Pallas kernels for 0% -> 11%
where the time goes in v1:
time: 115 us; the launch traced here: 114 us
  Pallas kernels  53.8 us (47%)
  starting transfers between devices  29.8 us (26%)
  waiting for transfers between devices  22.2 us (19%)
  local copies, waits for them, and re-layouts  5.3 us (5%)
  matrix products  1.79 us (2%)
    pallas_call x1, Pallas kernels, project_call(): pl.pallas_call(functools.partial(project_kernel, tile, tile_count), name=...  18.6 us
    pallas_call x1, Pallas kernels, cycle_call(): pl.pallas_call(cycle_kernel, name='cycle', in_specs=[smem, smem, vmem, vm...  11.7 us
    pallas_call x1, Pallas kernels, first_call(): pl.pallas_call(functools.partial(first_kernel, tile, len(pieces)), name='...  9.82 us
    ppermute x2, starting transfers between devices, halo_rows(): lax.ppermute(outer, 'tile', both[1])  8.52 us
    pallas_call x1, Pallas kernels, final_call(): pl.pallas_call(functools.partial(final_kernel, tile, len(old)), name='fin...  7.89 us
    all_to_all x1, starting transfers between devices, body(): lax.all_to_all(outgoing, 'tm', split_axis=0, concat_axis=0, tiled=True)  7.31 us
    ppermute x6, waiting for transfers between devices, gathered(): pieces[apart ^ step] = lax.ppermute(pieces[apart], 'tile', pairs)  5.94 us
    ppermute x2, waiting for transfers between devices, reduced(): lax.ppermute(send, 'tile', [(i, i ^ step) for i in range(peers)])  5.77 us
  transfers between devices with their start and end apart: 16, of which 9 were waited for; matrix products, arithmetic and copies ran while one was open for 2% of the time, Pallas kernels for 11%

profile of v1, /device:TPU:0, one launch (start us, length us, event | category | flops | bytes accessed | tf_op | source)
XLA Modules:
  0.0 114.2 jit_solution(10480403983806857335)
XLA Ops:
  0.6 0.0 copy-start.3
  0.6 0.0 copy-start.4
  0.7 1.7 %copy.10 = bf16[512,128]{1,0:T(8,128)(2,1)} copy(bf16[512,128]{0,1:T(8,128)(2,1)} %bitcast.38) | data formatting | bytes 262144 | tf_op jit(solution)/shard_map/transpose | solution.py:639
  2.3 7.3 %all-to-all-start = ((bf16[8,64,128]{2,1,0:T(8,128)(2,1)}), bf16[8,64,128]{2,1,0:T(8,128)(2,1)S(1)}, u32[]{:S(2)}, u32[]{:S(2)}) async-start(bf16[8,64,128]{2,1,0:T(8,128)(2,1)} %bitcast.6), calls=%async_computation | async-start | bytes 262144 | tf_op jit(solution)/shard_map/all_to_all | solution.py:640
  9.6 0.7 slice_bitcast_fusion
  10.3 0.1 fusion.11
  10.4 1.8 %convolution_convert_fusion = bf16[48,32,256]{2,1,0:T(8,128)(2,1)S(1)} fusion(f32[48,32,256]{2,1,0:T(8,128)} %param.12, pred[48,256]{1,0:T(8,128)(4,1)S(1)} %fusion.11, s32[256]{0:T(256)S(1)} %fusion.16), kind=kOutput, calls=%fused_computation.1 | convolution fusion | flops 202178560 | bytes 2372608 | tf_op jit(solution)/shard_map/dot_general | solution.py:633
  12.2 4.8 %all-to-all-done.refs_0_ = bf16[8,64,128]{2,1,0:T(8,128)(2,1)S(1)} async-done(((bf16[8,64,128]{2,1,0:T(8,128)(2,1)}), bf16[8,64,128]{2,1,0:T(8,128)(2,1)S(1)}, u32[]{:S(2)}, u32[]{:S(2)}) %all-to-all-start) | async-done | bytes 131104 | tf_op jit(solution)/shard_map/all_to_all | solution.py:640
  17.0 1.5 %collective-permute-start.1 = (bf16[8,64,128]{2,1,0:T(8,128)(2,1)S(1)}, bf16[8,64,128]{2,1,0:T(8,128)(2,1)S(1)}, u32[]{:S(2)}, u32[]{:S(2)}) collective-permute-start(bf16[8,64,128]{2,1,0:T(8,128)(2,1)S(1)} %all-to-all-done.refs_0_), channel_id=1, source_target_pairs={{0,16},{8,24},{16,0},{24,8},{1,17},{9,25},{17,1},{25,9},{2,18},{10... | collective-permute-start | bytes 393224 | tf_op jit(solution)/shard_map/ppermute | solution.py:555
  18.5 0.0 collective-permute-start
  18.5 3.5 %collective-permute-done.1.refs_2_ = bf16[8,64,128]{2,1,0:T(8,128)(2,1)S(1)} collective-permute-done((bf16[8,64,128]{2,1,0:T(8,128)(2,1)S(1)}, bf16[8,64,128]{2,1,0:T(8,128)(2,1)S(1)}, u32[]{:S(2)}, u32[]{:S(2)}) %collective-permute-start.1) | collective-permute-done | bytes 131104 | tf_op jit(solution)/shard_map/ppermute | solution.py:555
  21.9 0.0 collective-permute-start.2
  22.0 0.1 fusion.5
  22.1 0.0 collective-permute-done.refs_1_
  22.1 1.2 %collective-permute-done.2.refs_3_ = bf16[8,64,128]{2,1,0:T(8,128)(2,1)S(1)} collective-permute-done((bf16[8,64,128]{2,1,0:T(8,128)(2,1)S(1)}, bf16[8,64,128]{2,1,0:T(8,128)(2,1)S(1)}, u32[]{:S(2)}, u32[]{:S(2)}) %collective-permute-start.2) | collective-permute-done | bytes 131104 | tf_op jit(solution)/shard_map/ppermute | solution.py:555
  23.3 0.0 copy-done.3
  23.3 0.0 copy-done.4
  23.3 9.8 %first.1 = (bf16[32,64,256]{2,1,0:T(8,128)(2,1)}, bf16[8,64,256]{2,1,0:T(8,128)(2,1)S(1)}, bf16[8,64,256]{2,1,0:T(8,128)(2,1)}) custom-call(s32[4,8]{1,0:T(4,128)S(1)} %bitcast.21, s32[32]{0:T(128)S(1)} %copy-done.4, s32[1]{0:T(128)} %bitcast.1.here_ref, bf16[256,256]{1,0:T(8,128)(2,1)S(1)} %get-tuple-element.56.split_ref, bf16[32,64,256]{2,1,0:T(8,128)(2,1)} %bitcast.33, ...), custom_call_target="tpu_custom_call" | custom-call | tf_op jit(solution)/shard_map/first/pallas_call | solution.py:199
  33.1 0.7 collective-permute-start.3
  33.8 0.0 copy-start.2
  33.8 0.0 copy-start.5
  33.8 2.9 %collective-permute-start.4 = (bf16[8,64,256]{2,1,0:T(8,128)(2,1)}, bf16[8,64,256]{2,1,0:T(8,128)(2,1)S(1)}, u32[]{:S(2)}, u32[]{:S(2)}) collective-permute-start(bf16[8,64,256]{2,1,0:T(8,128)(2,1)} %get-tuple-element.31), channel_id=1, source_target_pairs={{0,8},{16,24},{8,0},{24,16},{1,9},{17,25},{9,1},{25,17},{2,10},{18... | collective-permute-start | bytes 786440 | tf_op jit(solution)/shard_map/ppermute | solution.py:395
  36.7 0.0 collective-permute-done.3.inner_ref
  36.7 1.4 %collective-permute-done.4.outer_ref = bf16[8,64,256]{2,1,0:T(8,128)(2,1)S(1)} collective-permute-done((bf16[8,64,256]{2,1,0:T(8,128)(2,1)}, bf16[8,64,256]{2,1,0:T(8,128)(2,1)S(1)}, u32[]{:S(2)}, u32[]{:S(2)}) %collective-permute-start.4) | collective-permute-done | bytes 262176 | tf_op jit(solution)/shard_map/ppermute | solution.py:395
  38.1 1.2 %broadcast_in_dim.16.weights_ref = bf16[48,32,8,256]{3,2,1,0:T(8,128)(2,1)S(1)} broadcast(bf16[48,32,256]{2,1,0:T(8,128)(2,1)S(1)} %convolution_convert_fusion), dimensions={0,1,3} | broadcast | bytes 7077888 | tf_op jit(solution)/shard_map/broadcast_in_dim | solution.py:650
  39.3 0.0 copy-start
  39.4 0.0 copy-done.2
  39.4 0.0 copy-done.5
  39.4 11.7 %cycle.1 = (bf16[32,64,256]{2,1,0:T(8,128)(2,1)S(1)}, bf16[8,64,256]{2,1,0:T(8,128)(2,1)S(1)}, bf16[8,64,256]{2,1,0:T(8,128)(2,1)S(1)}) custom-call(s32[2,48]{1,0:T(2,128)S(1)} %bitcast.25, s32[1]{0:T(128)} %bitcast.1.here_ref, bf16[8,64,256]{2,1,0:T(8,128)(2,1)S(1)} %collective-permute-done.3.inner_ref, ...), custom_call_target="tpu_custom_call" | custom-call | tf_op jit(solution)/shard_map/cycle/pallas_call | solution.py:374
  51.1 0.0 copy-done
  51.1 0.0 copy-start.1
  51.1 0.7 collective-permute-start.5
  51.8 5.6 %collective-permute-start.6 = (bf16[8,64,256]{2,1,0:T(8,128)(2,1)S(1)}, bf16[8,64,256]{2,1,0:T(8,128)(2,1)S(1)}, u32[]{:S(2)}, u32[]{:S(2)}) collective-permute-start(bf16[8,64,256]{2,1,0:T(8,128)(2,1)S(1)} %get-tuple-element.39), channel_id=1, source_target_pairs={{0,8},{16,24},{8,0},{24,16},{1,9},{17,25},{9,1},{25,17},{2,10},{18... | collective-permute-start | bytes 786440 | tf_op jit(solution)/shard_map/ppermute | solution.py:395
  57.4 4.2 %norms.1 = (f32[16,128]{1,0:T(8,128)S(1)}, bf16[32,128]{1,0:T(8,128)(2,1)S(1)}) custom-call(s32[4,8]{1,0:T(4,128)S(1)} %bitcast.22, s32[32]{0:T(128)S(1)} %copy-done.4, s32[1]{0:T(128)} %bitcast.1.here_ref, bf16[8,4,1024,128]{3,2,1,0:T(8,128)(2,1)} %bitcast.29), custom_call_target="tpu_custom_call" | custom-call | tf_op jit(solution)/shard_map/norms/pallas_call | solution.py:442
  61.6 0.0 copy-done.1
  61.6 0.0 collective-permute-done.5.inner_ref
  61.6 0.0 collective-permute-done.6.outer_ref
  61.7 18.6 %project.1 = (bf16[32,64,256]{2,1,0:T(8,128)(2,1)}, f32[16,64,128]{2,1,0:T(8,128)S(1)}, bf16[1056,128]{1,0:T(8,128)(2,1)S(1)}) custom-call(s32[4,8]{1,0:T(4,128)S(1)} %bitcast.23, s32[32]{0:T(128)S(1)} %copy-done.4, s32[2,48]{1,0:T(2,128)S(1)} %bitcast.26, s32[1]{0:T(128)} %bitcast.1.here_ref, bf16[256,256]{1,0:T(8,128)(2,1)S(1)} %get-tuple-element.57.join_ref, ...), custom_call_target="tpu_custom_call" | custom-call | tf_op jit(solution)/shard_map/project/pallas_call | solution.py:523
  80.3 0.1 collective-permute-start.7
  80.4 1.5 %collective-permute-done.7 = bf16[1056,128]{1,0:T(8,128)(2,1)S(1)} collective-permute-done((bf16[1056,128]{1,0:T(8,128)(2,1)S(1)}, bf16[1056,128]{1,0:T(8,128)(2,1)S(1)}, u32[]{:S(2)}, u32[]{:S(2)}) %collective-permute-start.7) | collective-permute-done | bytes 270368 | tf_op jit(solution)/shard_map/ppermute | solution.py:565
  82.0 0.1 add.102
  82.0 0.0 copy-start.7
  82.1 1.4 %collective-permute-start.8 = (bf16[528,128]{1,0:T(8,128)(2,1)S(1)}, bf16[528,128]{1,0:T(8,128)(2,1)S(1)}, u32[]{:S(2)}, u32[]{:S(2)}) collective-permute-start(bf16[528,128]{1,0:T(8,128)(2,1)S(1)} %pad_maximum_fusion), channel_id=1, source_target_pairs={{0,16},{8,24},{16,0},{24,8},{1,17},{9,25},{17,1},{25,9},{2,18},{10... | collective-permute-start | bytes 405512 | tf_op jit(solution)/shard_map/ppermute | solution.py:565
  83.6 4.3 %collective-permute-done.8 = bf16[528,128]{1,0:T(8,128)(2,1)S(1)} collective-permute-done((bf16[528,128]{1,0:T(8,128)(2,1)S(1)}, bf16[528,128]{1,0:T(8,128)(2,1)S(1)}, u32[]{:S(2)}, u32[]{:S(2)}) %collective-permute-start.8) | collective-permute-done | bytes 135200 | tf_op jit(solution)/shard_map/ppermute | solution.py:565
  87.9 0.1 fusion.18
  88.0 0.8 collective-permute-start.10
  88.8 2.6 %collective-permute-start.9 = (bf16[8,64,128]{2,1,0:T(8,128)(2,1)S(1)}, bf16[8,64,128]{2,1,0:T(8,128)(2,1)S(1)}, u32[]{:S(2)}, u32[]{:S(2)}) collective-permute-start(bf16[8,64,128]{2,1,0:T(8,128)(2,1)S(1)} %get-tuple-element.52), channel_id=1, source_target_pairs={{0,1},{1,0},{2,3},{3,2},{4,5},{5,4},{6,7},{7,6},{8,9},{9,8},{10,11... | collective-permute-start | bytes 393224 | tf_op jit(solution)/shard_map/ppermute | solution.py:668
  91.5 0.0 copy-done.7
  91.5 0.1 reverse
  91.6 0.1 slice.76
  91.6 0.0 collective-permute-done.10.other_ref
  91.6 4.3 %collective-permute-done.9.even_ref = bf16[8,64,128]{2,1,0:T(8,128)(2,1)S(1)} collective-permute-done((bf16[8,64,128]{2,1,0:T(8,128)(2,1)S(1)}, bf16[8,64,128]{2,1,0:T(8,128)(2,1)S(1)}, u32[]{:S(2)}, u32[]{:S(2)}) %collective-permute-start.9) | collective-permute-done | bytes 131104 | tf_op jit(solution)/shard_map/ppermute | solution.py:668
  96.0 1.5 %wiener.1.refs_4_ = bf16[8,64,128]{2,1,0:T(8,128)(2,1)} custom-call(s32[1]{0:T(128)} %bitcast.9.odd_ref, f32[1,256]{1,0:T(1,128)S(1)} %bitcast.27, f32[8,64,128]{2,1,0:T(8,128)S(1)} %get-tuple-element.53.own_ref, bf16[8,64,128]{2,1,0:T(8,128)(2,1)S(1)} %collective-permute-done.9.even_ref, bf16[8,64,128]{2,1,0:T(8,128)(2,1)S(1)} %collective-permute-done.10.other_ref), custom_call_target="tpu_custom_call" | custom-call | tf_op jit(solution)/shard_map/wiener/pallas_call | solution.py:605
  97.5 1.4 %collective-permute-start.12 = (bf16[8,64,128]{2,1,0:T(8,128)(2,1)}, bf16[8,64,128]{2,1,0:T(8,128)(2,1)S(1)}, u32[]{:S(2)}, u32[]{:S(2)}) collective-permute-start(bf16[8,64,128]{2,1,0:T(8,128)(2,1)} %wiener.1.refs_4_), channel_id=1, source_target_pairs={{0,16},{8,24},{16,0},{24,8},{1,17},{9,25},{17,1},{25,9},{2,18},{10... | collective-permute-start | bytes 393224 | tf_op jit(solution)/shard_map/ppermute | solution.py:555
  98.9 4.3 %all-to-all-start.1 = ((bf16[8,64,128]{2,1,0:T(8,128)(2,1)}), bf16[8,64,128]{2,1,0:T(8,128)(2,1)S(1)}, u32[]{:S(2)}, u32[]{:S(2)}) async-start(bf16[8,64,128]{2,1,0:T(8,128)(2,1)} %wiener.1.refs_4_), calls=%async_computation.1 | async-start | bytes 262144 | tf_op jit(solution)/shard_map/all_to_all | solution.py:676
  103.2 0.0 collective-permute-start.11
  103.2 0.0 collective-permute-done.12.refs_6_
  103.2 0.5 collective-permute-start.13
  103.7 1.0 collective-permute-done.11.refs_5_
  104.7 0.2 collective-permute-done.13.refs_7_
  104.9 0.7 copy-done.6
  105.6 7.9 %final.1 = bf16[32,64,256]{2,1,0:T(8,128)(2,1)} custom-call(s32[4,8]{1,0:T(4,128)S(1)} %bitcast.24, s32[32]{0:T(128)S(1)} %copy-done.4, s32[1]{0:T(128)} %bitcast.1.here_ref, bf16[32,64,256]{2,1,0:T(8,128)(2,1)} %get-tuple-element.46.third_ref, bf16[8,4,1024,128]{3,2,1,0:T(8,128)(2,1)} %bitcast.31, bf16[8,64,128]{2,1,0:T(8,128)(2,1)S(1)} %all-to-all-done.refs_0_, ...), custom_call_target="tpu_custom_call" | custom-call | tf_op jit(solution)/shard_map/final/pallas_call | solution.py:252
  113.5 0.0 all-to-all-done.1
  113.5 0.8 copy.11
  (12 shorter events, 0.2 us)
Async XLA Ops:
  0.6 22.7 %copy-start.3 = (s32[8,4]{0,1:T(4,128)S(1)}, s32[8,4]{0,1:T(4,128)}, u32[]{:S(2)}) copy-start(s32[8,4]{0,1:T(4,128)} %param.10) | copy-start | bytes 388
  0.6 22.7 %copy-start.4 = (s32[32]{0:T(128)S(1)}, s32[32]{0:T(128)}, u32[]{:S(2)}) copy-start(s32[32]{0:T(128)} %owner_ref.7) | copy-start | bytes 388
  2.3 14.7 %all-to-all-start = ((bf16[8,64,128]{2,1,0:T(8,128)(2,1)}), bf16[8,64,128]{2,1,0:T(8,128)(2,1)S(1)}, u32[]{:S(2)}, u32[]{:S(2)}) async-start(bf16[8,64,128]{2,1,0:T(8,128)(2,1)} %bitcast.6), calls=%async_computation | async-start | bytes 262144 | tf_op jit(solution)/shard_map/all_to_all | solution.py:640
  17.0 5.0 %collective-permute-start.1 = (bf16[8,64,128]{2,1,0:T(8,128)(2,1)S(1)}, bf16[8,64,128]{2,1,0:T(8,128)(2,1)S(1)}, u32[]{:S(2)}, u32[]{:S(2)}) collective-permute-start(bf16[8,64,128]{2,1,0:T(8,128)(2,1)S(1)} %all-to-all-done.refs_0_), channel_id=1, source_target_pairs={{0,16},{8,24},{16,0},{24,8},{1,17},{9,25},{17,1},{25,9},{2,18},{10... | collective-permute-start | bytes 393224 | tf_op jit(solution)/shard_map/ppermute | solution.py:555
  18.5 3.6 %collective-permute-start = (bf16[8,64,128]{2,1,0:T(8,128)(2,1)S(1)}, bf16[8,64,128]{2,1,0:T(8,128)(2,1)S(1)}, u32[]{:S(2)}, u32[]{:S(2)}) collective-permute-start(bf16[8,64,128]{2,1,0:T(8,128)(2,1)S(1)} %all-to-all-done.refs_0_), channel_id=1, source_target_pairs={{0,8},{8,0},{16,24},{24,16},{1,9},{9,1},{17,25},{25,17},{2,10},{10... | collective-permute-start | bytes 393224 | tf_op jit(solution)/shard_map/ppermute | solution.py:555
  21.9 1.3 %collective-permute-start.2 = (bf16[8,64,128]{2,1,0:T(8,128)(2,1)S(1)}, bf16[8,64,128]{2,1,0:T(8,128)(2,1)S(1)}, u32[]{:S(2)}, u32[]{:S(2)}) collective-permute-start(bf16[8,64,128]{2,1,0:T(8,128)(2,1)S(1)} %collective-permute-done.1.refs_2_), channel_id=1, source_target_pairs={{0,8},{8,0},{16,24},{24,16},{1,9},{9,1},{17,25},{25,17},{2,10},{10... | collective-permute-start | bytes 393224 | tf_op jit(solution)/shard_map/ppermute | solution.py:555
  33.1 3.6 %collective-permute-start.3 = (bf16[8,64,256]{2,1,0:T(8,128)(2,1)S(1)}, bf16[8,64,256]{2,1,0:T(8,128)(2,1)S(1)}, u32[]{:S(2)}, u32[]{:S(2)}) collective-permute-start(bf16[8,64,256]{2,1,0:T(8,128)(2,1)S(1)} %get-tuple-element.30), channel_id=1, source_target_pairs={{8,16},{16,8},{9,17},{17,9},{10,18},{18,10},{11,19},{19,11},{12,20... | collective-permute-start | bytes 786440 | tf_op jit(solution)/shard_map/ppermute | solution.py:395
  33.8 5.5 %copy-start.2 = (bf16[32,64,256]{2,1,0:T(8,128)(2,1)S(1)}, bf16[32,64,256]{2,1,0:T(8,128)(2,1)}, u32[]{:S(2)}) copy-start(bf16[32,64,256]{2,1,0:T(8,128)(2,1)} %get-tuple-element.35.field_ref) | copy-start | bytes 3145732
  33.8 5.5 %copy-start.5 = (s32[48,2]{0,1:T(2,128)S(1)}, s32[48,2]{0,1:T(2,128)}, u32[]{:S(2)}) copy-start(s32[48,2]{0,1:T(2,128)} %param.11) | copy-start | bytes 1156
  33.8 4.3 %collective-permute-start.4 = (bf16[8,64,256]{2,1,0:T(8,128)(2,1)}, bf16[8,64,256]{2,1,0:T(8,128)(2,1)S(1)}, u32[]{:S(2)}, u32[]{:S(2)}) collective-permute-start(bf16[8,64,256]{2,1,0:T(8,128)(2,1)} %get-tuple-element.31), channel_id=1, source_target_pairs={{0,8},{16,24},{8,0},{24,16},{1,9},{17,25},{9,1},{25,17},{2,10},{18... | collective-permute-start | bytes 786440 | tf_op jit(solution)/shard_map/ppermute | solution.py:395
  39.3 11.8 %copy-start = (bf16[48,32,8,256]{3,2,1,0:T(8,128)(2,1)}, bf16[48,32,8,256]{3,2,1,0:T(8,128)(2,1)S(1)}, u32[]{:S(2)}) copy-start(bf16[48,32,8,256]{3,2,1,0:T(8,128)(2,1)S(1)} %broadcast_in_dim.16.weights_ref) | copy-start | bytes 18874372
  51.1 10.5 %copy-start.1 = (bf16[32,64,256]{2,1,0:T(8,128)(2,1)}, bf16[32,64,256]{2,1,0:T(8,128)(2,1)S(1)}, u32[]{:S(2)}) copy-start(bf16[32,64,256]{2,1,0:T(8,128)(2,1)S(1)} %get-tuple-element.44.field_ref) | copy-start | bytes 3145732
  51.1 10.5 %collective-permute-start.5 = (bf16[8,64,256]{2,1,0:T(8,128)(2,1)S(1)}, bf16[8,64,256]{2,1,0:T(8,128)(2,1)S(1)}, u32[]{:S(2)}, u32[]{:S(2)}) collective-permute-start(bf16[8,64,256]{2,1,0:T(8,128)(2,1)S(1)} %get-tuple-element.38), channel_id=1, source_target_pairs={{8,16},{16,8},{9,17},{17,9},{10,18},{18,10},{11,19},{19,11},{12,20... | collective-permute-start | bytes 786440 | tf_op jit(solution)/shard_map/ppermute | solution.py:395
  51.8 9.8 %collective-permute-start.6 = (bf16[8,64,256]{2,1,0:T(8,128)(2,1)S(1)}, bf16[8,64,256]{2,1,0:T(8,128)(2,1)S(1)}, u32[]{:S(2)}, u32[]{:S(2)}) collective-permute-start(bf16[8,64,256]{2,1,0:T(8,128)(2,1)S(1)} %get-tuple-element.39), channel_id=1, source_target_pairs={{0,8},{16,24},{8,0},{24,16},{1,9},{17,25},{9,1},{25,17},{2,10},{18... | collective-permute-start | bytes 786440 | tf_op jit(solution)/shard_map/ppermute | solution.py:395
  80.3 1.6 %collective-permute-start.7 = (bf16[1056,128]{1,0:T(8,128)(2,1)S(1)}, bf16[1056,128]{1,0:T(8,128)(2,1)S(1)}, u32[]{:S(2)}, u32[]{:S(2)}) collective-permute-start(bf16[1056,128]{1,0:T(8,128)(2,1)S(1)} %get-tuple-element.48), channel_id=1, source_target_pairs={{0,8},{8,0},{16,24},{24,16},{1,9},{9,1},{17,25},{25,17},{2,10},{10... | collective-permute-start | bytes 811016 | tf_op jit(solution)/shard_map/ppermute | solution.py:565
  82.0 9.4 %copy-start.7 = (f32[129]{0:T(256)S(1)}, f32[129]{0:T(256)}, u32[]{:S(2)}) copy-start(f32[129]{0:T(256)} %param.15) | copy-start | bytes 1552
  82.1 5.7 %collective-permute-start.8 = (bf16[528,128]{1,0:T(8,128)(2,1)S(1)}, bf16[528,128]{1,0:T(8,128)(2,1)S(1)}, u32[]{:S(2)}, u32[]{:S(2)}) collective-permute-start(bf16[528,128]{1,0:T(8,128)(2,1)S(1)} %pad_maximum_fusion), channel_id=1, source_target_pairs={{0,16},{8,24},{16,0},{24,8},{1,17},{9,25},{17,1},{25,9},{2,18},{10... | collective-permute-start | bytes 405512 | tf_op jit(solution)/shard_map/ppermute | solution.py:565
  88.0 3.7 %collective-permute-start.10 = (bf16[8,64,128]{2,1,0:T(8,128)(2,1)S(1)}, bf16[8,64,128]{2,1,0:T(8,128)(2,1)S(1)}, u32[]{:S(2)}, u32[]{:S(2)}) collective-permute-start(bf16[8,64,128]{2,1,0:T(8,128)(2,1)S(1)} %get-tuple-element.52), channel_id=1, source_target_pairs={{1,2},{3,4},{5,6},{2,1},{4,3},{6,5},{9,10},{11,12},{13,14},{10,9},... | collective-permute-start | bytes 393224 | tf_op jit(solution)/shard_map/ppermute | solution.py:669
  88.8 7.2 %collective-permute-start.9 = (bf16[8,64,128]{2,1,0:T(8,128)(2,1)S(1)}, bf16[8,64,128]{2,1,0:T(8,128)(2,1)S(1)}, u32[]{:S(2)}, u32[]{:S(2)}) collective-permute-start(bf16[8,64,128]{2,1,0:T(8,128)(2,1)S(1)} %get-tuple-element.52), channel_id=1, source_target_pairs={{0,1},{1,0},{2,3},{3,2},{4,5},{5,4},{6,7},{7,6},{8,9},{9,8},{10,11... | collective-permute-start | bytes 393224 | tf_op jit(solution)/shard_map/ppermute | solution.py:668
  97.5 5.7 %collective-permute-start.12 = (bf16[8,64,128]{2,1,0:T(8,128)(2,1)}, bf16[8,64,128]{2,1,0:T(8,128)(2,1)S(1)}, u32[]{:S(2)}, u32[]{:S(2)}) collective-permute-start(bf16[8,64,128]{2,1,0:T(8,128)(2,1)} %wiener.1.refs_4_), channel_id=1, source_target_pairs={{0,16},{8,24},{16,0},{24,8},{1,17},{9,25},{17,1},{25,9},{2,18},{10... | collective-permute-start | bytes 393224 | tf_op jit(solution)/shard_map/ppermute | solution.py:555
  98.9 14.6 %all-to-all-start.1 = ((bf16[8,64,128]{2,1,0:T(8,128)(2,1)}), bf16[8,64,128]{2,1,0:T(8,128)(2,1)S(1)}, u32[]{:S(2)}, u32[]{:S(2)}) async-start(bf16[8,64,128]{2,1,0:T(8,128)(2,1)} %wiener.1.refs_4_), calls=%async_computation.1 | async-start | bytes 262144 | tf_op jit(solution)/shard_map/all_to_all | solution.py:676
  103.2 1.6 %collective-permute-start.11 = (bf16[8,64,128]{2,1,0:T(8,128)(2,1)}, bf16[8,64,128]{2,1,0:T(8,128)(2,1)S(1)}, u32[]{:S(2)}, u32[]{:S(2)}) collective-permute-start(bf16[8,64,128]{2,1,0:T(8,128)(2,1)} %wiener.1.refs_4_), channel_id=1, source_target_pairs={{0,8},{8,0},{16,24},{24,16},{1,9},{9,1},{17,25},{25,17},{2,10},{10... | collective-permute-start | bytes 393224 | tf_op jit(solution)/shard_map/ppermute | solution.py:555
  103.2 1.7 %collective-permute-start.13 = (bf16[8,64,128]{2,1,0:T(8,128)(2,1)S(1)}, bf16[8,64,128]{2,1,0:T(8,128)(2,1)S(1)}, u32[]{:S(2)}, u32[]{:S(2)}) collective-permute-start(bf16[8,64,128]{2,1,0:T(8,128)(2,1)S(1)} %collective-permute-done.12.refs_6_), channel_id=1, source_target_pairs={{0,8},{8,0},{16,24},{24,16},{1,9},{9,1},{17,25},{25,17},{2,10},{10... | collective-permute-start | bytes 393224 | tf_op jit(solution)/shard_map/ppermute | solution.py:555
  104.9 0.7 copy-start.6

commit v2 on v1

--- a/solution.py
+++ b/solution.py
@@ -10,7 +10,7 @@
 RAD = 8
 LANES = 128
 ROW_STEP = 8
-AHEAD = 4
+AHEAD = 2
 FIRST_VMEM = 53
 FINAL_VMEM = 53
 TAP_GROUP = 4
@@ -385,6 +385,30 @@
         ],
         compiler_params=pltpu.CompilerParams(vmem_limit_bytes=40 * MIB),
     )(offsets, here, inner, outer, field, weights)
+
+
+def spread_kernel(weights_ref, out_ref):
+    taps, rows, sublanes, cols = out_ref.shape
+
+    def step(y, carry):
+        for j in range(taps):
+            row = jnp.broadcast_to(weights_ref[j, pl.ds(y, 1), :], (sublanes, cols))
+            out_ref[j, y] = row.astype(bf16)
+        return carry
+
+    lax.fori_loop(0, rows, step, 0)
+
+
+def spread_call(weights):
+    shape = weights.shape[:2] + (8,) + weights.shape[2:]
+    return pl.pallas_call(
+        spread_kernel,
+        name="spread",
+        in_specs=[vmem],
+        out_specs=vmem,
+        out_shape=jax.ShapeDtypeStruct(shape, bf16),
+        compiler_params=pltpu.CompilerParams(vmem_limit_bytes=2 * MIB),
+    )(weights)
 
 
 def halo_rows(inner, outer):
@@ -629,10 +653,6 @@
     join = (source[:, None] == columns[None, :]).astype(bf16)
     reached = columns[None, :] + cycle_offsets[:, 1:2]
     inside = (reached >= 0) & (reached < cols)
-    weights = jnp.where(inside[:, None, :], cycle_weights, 0.0).astype(bf16)
-    weights = lax.dot_general(
-        weights, split, (((2,), (0,)), ((), ())), preferred_element_type=f32
-    ).astype(bf16)
     offsets, slots_held = cycle_offsets.T, support.T
     here = tile_here.astype(jnp.int32).reshape(1)
 
@@ -641,19 +661,21 @@
     pieces = block // owned
     group_old = group_old.reshape(share, pieces, frames, owned).transpose(0, 2, 1, 3)
     group_old = group_old.reshape(share, frames, block)
-    group_old, weights = lax.optimization_barrier((group_old, weights))
+    norms, norms_away = norm_call(slots_held, owner_map, here, prints, tile_count)
+    group_old, norms_away = lax.optimization_barrier((group_old, norms_away))
     old = gathered(group_old)
 
     first_res, inner, outer = first_call(slots_held, owner_map, here, split, field, prints, old)
-    inner, weights = lax.optimization_barrier((inner, weights))
+    inner, cycle_weights = lax.optimization_barrier((inner, cycle_weights))
     inner, outer = halo_rows(inner, outer)
-    weights = jnp.broadcast_to(weights[:, :, None, :], weights.shape[:2] + (8, cols))
+    weights = jnp.where(inside[:, None, :], cycle_weights, 0.0).astype(bf16)
+    weights = lax.dot_general(
+        weights, split, (((2,), (0,)), ((), ())), preferred_element_type=f32
+    )
+    weights = spread_call(weights)
     inner, outer, weights = lax.optimization_barrier((inner, outer, weights))
     second_res, inner, outer = cycle_call(offsets, here, inner, outer, first_res, weights)
-    inner, tied = lax.optimization_barrier((inner, prints))
     inner, outer = halo_rows(inner, outer)
-    norms, norms_away = norm_call(slots_held, owner_map, here, tied, tile_count)
-    inner, outer, norms_away = lax.optimization_barrier((inner, outer, norms_away))
     third_res, keep, send = project_call(
         slots_held, owner_map, offsets, here, join, inner, outer, second_res, norms_away, weights,
         prints, tile_count,

time: 115 us -> 115 us (level)
  starting transfers between devices: 29.8 us -> 34.5 us
  waiting for transfers between devices: 22.2 us -> 18.5 us
  matrix products: 1.79 us -> 0.38 us
    ppermute x2, starting transfers between devices: 1.53 us -> 4.95 us  [reduced(): lax.ppermute(send, 'tile', [(i, i ^ step) for i in range(peers)])]
    all_to_all x1, waiting for transfers between devices: 4.77 us -> 1.7 us  [body(): lax.all_to_all(outgoing, 'tm', split_axis=0, concat_axis=0, tiled=True)]
    unnamed x18 -> x24, local copies, waits for them, and re-layouts: 0.86 us -> 3.27 us
    dot_general x1, matrix products: 1.79 us -> 0.38 us  [body(): lax.dot_general(weights, split, (((2,), (0,)), ((), ())), preferred_eleme...]
    all_to_all x1, starting transfers between devices: 4.29 us -> 5.56 us  [body(): lax.all_to_all(leaving, 'tm', split_axis=0, concat_axis=0, tiled=True)]
    broadcast_in_dim x1 -> x0, local copies, waits for them, and re-layouts: 1.23 us -> none  [body(): jnp.broadcast_to(weights[:, :, None, :], weights.shape[:2] + (8, cols))]
  transfers between devices with their start and end apart: 16 -> 16, of which waited for: 9 -> 9; matrix products, arithmetic and copies ran while one was open for 2% -> 1% of each run, Pallas kernels for 11% -> 11%
where the time goes in v2:
time: 115 us; the launch traced here: 114 us
  Pallas kernels  53.7 us (47%)
  starting transfers between devices  34.5 us (30%)
  waiting for transfers between devices  18.5 us (16%)
  local copies, waits for them, and re-layouts  5.79 us (5%)
    pallas_call x1, Pallas kernels, project_call(): pl.pallas_call(functools.partial(project_kernel, tile, tile_count), name=...  18.6 us
    pallas_call x1, Pallas kernels, cycle_call(): pl.pallas_call(cycle_kernel, name='cycle', in_specs=[smem, smem, vmem, vm...  11.7 us
    pallas_call x1, Pallas kernels, first_call(): pl.pallas_call(functools.partial(first_kernel, tile, len(pieces)), name='...  8.77 us
    ppermute x2, starting transfers between devices, halo_rows(): lax.ppermute(outer, 'tile', both[1])  8.31 us
    pallas_call x1, Pallas kernels, final_call(): pl.pallas_call(functools.partial(final_kernel, tile, len(old)), name='fin...  7.92 us
    all_to_all x1, starting transfers between devices, body(): lax.all_to_all(outgoing, 'tm', split_axis=0, concat_axis=0, tiled=True)  7.31 us
    ppermute x6, waiting for transfers between devices, gathered(): pieces[apart ^ step] = lax.ppermute(pieces[apart], 'tile', pairs)  5.95 us
    all_to_all x1, starting transfers between devices, body(): lax.all_to_all(leaving, 'tm', split_axis=0, concat_axis=0, tiled=True)  5.56 us
  transfers between devices with their start and end apart: 16, of which 9 were waited for; matrix products, arithmetic and copies ran while one was open for 1% of the time, Pallas kernels for 11%

profile of v2, /device:TPU:0, one launch (start us, length us, event | category | flops | bytes accessed | tf_op | source)
XLA Modules:
  0.0 114.3 jit_solution(7281376089086742793)
XLA Ops:
  0.6 1.7 %copy.10 = bf16[512,128]{1,0:T(8,128)(2,1)} copy(bf16[512,128]{0,1:T(8,128)(2,1)} %bitcast.38) | data formatting | bytes 262144 | tf_op jit(solution)/shard_map/transpose | solution.py:659
  2.3 7.3 %all-to-all-start = ((bf16[8,64,128]{2,1,0:T(8,128)(2,1)}), bf16[8,64,128]{2,1,0:T(8,128)(2,1)S(1)}, u32[]{:S(2)}, u32[]{:S(2)}) async-start(bf16[8,64,128]{2,1,0:T(8,128)(2,1)} %bitcast.6), calls=%async_computation | async-start | bytes 262144 | tf_op jit(solution)/shard_map/all_to_all | solution.py:660
  9.6 0.0 copy-start.3
  9.6 0.7 copy-done.3
  10.3 0.7 copy-done.5
  11.0 4.2 %norms.1 = (f32[16,128]{1,0:T(8,128)S(1)}, bf16[32,128]{1,0:T(8,128)(2,1)S(1)}) custom-call(s32[4,8]{1,0:T(4,128)S(1)} %bitcast.21, s32[32]{0:T(128)S(1)} %copy-done.5, s32[1]{0:T(128)} %bitcast.1.here_ref, bf16[8,4,1024,128]{3,2,1,0:T(8,128)(2,1)} %bitcast.28), custom_call_target="tpu_custom_call" | custom-call | tf_op jit(solution)/shard_map/norms/pallas_call | solution.py:466
  15.1 0.1 fusion.6
  15.2 1.7 %all-to-all-done.refs_0_ = bf16[8,64,128]{2,1,0:T(8,128)(2,1)S(1)} async-done(((bf16[8,64,128]{2,1,0:T(8,128)(2,1)}), bf16[8,64,128]{2,1,0:T(8,128)(2,1)S(1)}, u32[]{:S(2)}, u32[]{:S(2)}) %all-to-all-start) | async-done | bytes 131104 | tf_op jit(solution)/shard_map/all_to_all | solution.py:660
  16.9 1.5 %collective-permute-start.1 = (bf16[8,64,128]{2,1,0:T(8,128)(2,1)S(1)}, bf16[8,64,128]{2,1,0:T(8,128)(2,1)S(1)}, u32[]{:S(2)}, u32[]{:S(2)}) collective-permute-start(bf16[8,64,128]{2,1,0:T(8,128)(2,1)S(1)} %all-to-all-done.refs_0_), channel_id=1, source_target_pairs={{0,16},{8,24},{16,0},{24,8},{1,17},{9,25},{17,1},{25,9},{2,18},{10... | collective-permute-start | bytes 393224 | tf_op jit(solution)/shard_map/ppermute | solution.py:579
  18.4 0.0 copy-done.7
  18.4 0.0 collective-permute-start
  18.5 3.5 %collective-permute-done.1.refs_2_ = bf16[8,64,128]{2,1,0:T(8,128)(2,1)S(1)} collective-permute-done((bf16[8,64,128]{2,1,0:T(8,128)(2,1)S(1)}, bf16[8,64,128]{2,1,0:T(8,128)(2,1)S(1)}, u32[]{:S(2)}, u32[]{:S(2)}) %collective-permute-start.1) | collective-permute-done | bytes 131104 | tf_op jit(solution)/shard_map/ppermute | solution.py:579
  21.9 0.0 collective-permute-start.2
  21.9 0.1 fusion.12
  22.0 0.0 collective-permute-done.refs_1_
  22.0 1.2 %collective-permute-done.2.refs_3_ = bf16[8,64,128]{2,1,0:T(8,128)(2,1)S(1)} collective-permute-done((bf16[8,64,128]{2,1,0:T(8,128)(2,1)S(1)}, bf16[8,64,128]{2,1,0:T(8,128)(2,1)S(1)}, u32[]{:S(2)}, u32[]{:S(2)}) %collective-permute-start.2) | collective-permute-done | bytes 131104 | tf_op jit(solution)/shard_map/ppermute | solution.py:579
  23.3 0.0 copy-done.4
  23.3 0.0 copy-done.6
  23.3 8.8 %first.1 = (bf16[32,64,256]{2,1,0:T(8,128)(2,1)}, bf16[8,64,256]{2,1,0:T(8,128)(2,1)S(1)}, bf16[8,64,256]{2,1,0:T(8,128)(2,1)}) custom-call(s32[4,8]{1,0:T(4,128)S(1)} %bitcast.22, s32[32]{0:T(128)S(1)} %copy-done.6, s32[1]{0:T(128)} %bitcast.1.here_ref, bf16[256,256]{1,0:T(8,128)(2,1)S(1)} %get-tuple-element.46.split_ref, bf16[32,64,256]{2,1,0:T(8,128)(2,1)} %bitcast.33, ...), custom_call_target="tpu_custom_call" | custom-call | tf_op jit(solution)/shard_map/first/pallas_call | solution.py:199
  32.0 0.7 collective-permute-start.3
  32.7 2.9 %collective-permute-start.4 = (bf16[8,64,256]{2,1,0:T(8,128)(2,1)}, bf16[8,64,256]{2,1,0:T(8,128)(2,1)S(1)}, u32[]{:S(2)}, u32[]{:S(2)}) collective-permute-start(bf16[8,64,256]{2,1,0:T(8,128)(2,1)} %get-tuple-element.26), channel_id=1, source_target_pairs={{0,8},{16,24},{8,0},{24,16},{1,9},{17,25},{9,1},{25,17},{2,10},{18... | collective-permute-start | bytes 786440 | tf_op jit(solution)/shard_map/ppermute | solution.py:419
  35.6 0.0 copy-done.8
  35.6 0.4 fusion.weights_ref
  36.0 0.0 copy-start.2
  36.0 1.0 spread.1.weights_ref
  37.1 0.0 copy-start
  37.1 0.0 collective-permute-done.3.inner_ref
  37.1 0.0 collective-permute-done.4.outer_ref
  37.1 0.1 copy-done.2
  37.3 11.7 %cycle.1 = (bf16[32,64,256]{2,1,0:T(8,128)(2,1)S(1)}, bf16[8,64,256]{2,1,0:T(8,128)(2,1)S(1)}, bf16[8,64,256]{2,1,0:T(8,128)(2,1)S(1)}) custom-call(s32[2,48]{1,0:T(2,128)S(1)} %bitcast.25, s32[1]{0:T(128)} %bitcast.1.here_ref, bf16[8,64,256]{2,1,0:T(8,128)(2,1)S(1)} %collective-permute-done.3.inner_ref, ...), custom_call_target="tpu_custom_call" | custom-call | tf_op jit(solution)/shard_map/cycle/pallas_call | solution.py:374
  49.0 0.0 copy-done
  49.0 0.0 copy-start.1
  49.0 1.0 copy-done.1
  50.0 0.7 collective-permute-start.5
  50.6 5.4 %collective-permute-start.6 = (bf16[8,64,256]{2,1,0:T(8,128)(2,1)S(1)}, bf16[8,64,256]{2,1,0:T(8,128)(2,1)S(1)}, u32[]{:S(2)}, u32[]{:S(2)}) collective-permute-start(bf16[8,64,256]{2,1,0:T(8,128)(2,1)S(1)} %get-tuple-element.33), channel_id=1, source_target_pairs={{0,8},{16,24},{8,0},{24,16},{1,9},{17,25},{9,1},{25,17},{2,10},{18... | collective-permute-start | bytes 786440 | tf_op jit(solution)/shard_map/ppermute | solution.py:419
  56.0 0.0 collective-permute-done.5.inner_ref
  56.0 1.2 %collective-permute-done.6.outer_ref = bf16[8,64,256]{2,1,0:T(8,128)(2,1)S(1)} collective-permute-done((bf16[8,64,256]{2,1,0:T(8,128)(2,1)S(1)}, bf16[8,64,256]{2,1,0:T(8,128)(2,1)S(1)}, u32[]{:S(2)}, u32[]{:S(2)}) %collective-permute-start.6) | collective-permute-done | bytes 262176 | tf_op jit(solution)/shard_map/ppermute | solution.py:419
  57.2 18.6 %project.1 = (bf16[32,64,256]{2,1,0:T(8,128)(2,1)}, f32[16,64,128]{2,1,0:T(8,128)S(1)}, bf16[1056,128]{1,0:T(8,128)(2,1)S(1)}) custom-call(s32[4,8]{1,0:T(4,128)S(1)} %bitcast.23, s32[32]{0:T(128)S(1)} %copy-done.6, s32[2,48]{1,0:T(2,128)S(1)} %bitcast.26, s32[1]{0:T(128)} %bitcast.1.here_ref, bf16[256,256]{1,0:T(8,128)(2,1)S(1)} %get-tuple-element.47.join_ref, ...), custom_call_target="tpu_custom_call" | custom-call | tf_op jit(solution)/shard_map/project/pallas_call | solution.py:547
  75.8 3.1 %collective-permute-start.7 = (bf16[1056,128]{1,0:T(8,128)(2,1)S(1)}, bf16[1056,128]{1,0:T(8,128)(2,1)S(1)}, u32[]{:S(2)}, u32[]{:S(2)}) collective-permute-start(bf16[1056,128]{1,0:T(8,128)(2,1)S(1)} %get-tuple-element.38), channel_id=1, source_target_pairs={{0,8},{8,0},{16,24},{24,16},{1,9},{9,1},{17,25},{25,17},{2,10},{10... | collective-permute-start | bytes 811016 | tf_op jit(solution)/shard_map/ppermute | solution.py:589
  79.0 1.2 %collective-permute-done.7 = bf16[1056,128]{1,0:T(8,128)(2,1)S(1)} collective-permute-done((bf16[1056,128]{1,0:T(8,128)(2,1)S(1)}, bf16[1056,128]{1,0:T(8,128)(2,1)S(1)}, u32[]{:S(2)}, u32[]{:S(2)}) %collective-permute-start.7) | collective-permute-done | bytes 270368 | tf_op jit(solution)/shard_map/ppermute | solution.py:589
  80.2 0.1 add.102
  80.3 0.0 copy-start.10
  80.4 1.8 %collective-permute-start.8 = (bf16[528,128]{1,0:T(8,128)(2,1)S(1)}, bf16[528,128]{1,0:T(8,128)(2,1)S(1)}, u32[]{:S(2)}, u32[]{:S(2)}) collective-permute-start(bf16[528,128]{1,0:T(8,128)(2,1)S(1)} %pad_maximum_fusion), channel_id=1, source_target_pairs={{0,16},{8,24},{16,0},{24,8},{1,17},{9,25},{17,1},{25,9},{2,18},{10... | collective-permute-start | bytes 405512 | tf_op jit(solution)/shard_map/ppermute | solution.py:589
  82.2 4.1 %collective-permute-done.8 = bf16[528,128]{1,0:T(8,128)(2,1)S(1)} collective-permute-done((bf16[528,128]{1,0:T(8,128)(2,1)S(1)}, bf16[528,128]{1,0:T(8,128)(2,1)S(1)}, u32[]{:S(2)}, u32[]{:S(2)}) %collective-permute-start.8) | collective-permute-done | bytes 135200 | tf_op jit(solution)/shard_map/ppermute | solution.py:589
  86.4 0.1 fusion.19
  86.5 0.7 collective-permute-start.10
  87.1 3.2 %collective-permute-start.9 = (bf16[8,64,128]{2,1,0:T(8,128)(2,1)S(1)}, bf16[8,64,128]{2,1,0:T(8,128)(2,1)S(1)}, u32[]{:S(2)}, u32[]{:S(2)}) collective-permute-start(bf16[8,64,128]{2,1,0:T(8,128)(2,1)S(1)} %get-tuple-element.42), channel_id=1, source_target_pairs={{0,1},{1,0},{2,3},{3,2},{4,5},{5,4},{6,7},{7,6},{8,9},{9,8},{10,11... | collective-permute-start | bytes 393224 | tf_op jit(solution)/shard_map/ppermute | solution.py:690
  90.3 0.0 copy-done.10
  90.3 0.1 reverse
  90.4 0.1 slice.76
  90.5 0.0 collective-permute-done.10.other_ref
  90.5 4.4 %collective-permute-done.9.even_ref = bf16[8,64,128]{2,1,0:T(8,128)(2,1)S(1)} collective-permute-done((bf16[8,64,128]{2,1,0:T(8,128)(2,1)S(1)}, bf16[8,64,128]{2,1,0:T(8,128)(2,1)S(1)}, u32[]{:S(2)}, u32[]{:S(2)}) %collective-permute-start.9) | collective-permute-done | bytes 131104 | tf_op jit(solution)/shard_map/ppermute | solution.py:690
  94.9 1.5 %wiener.1.refs_4_ = bf16[8,64,128]{2,1,0:T(8,128)(2,1)} custom-call(s32[1]{0:T(128)} %bitcast.9.odd_ref, f32[1,256]{1,0:T(1,128)S(1)} %bitcast.27, f32[8,64,128]{2,1,0:T(8,128)S(1)} %get-tuple-element.43.own_ref, bf16[8,64,128]{2,1,0:T(8,128)(2,1)S(1)} %collective-permute-done.9.even_ref, bf16[8,64,128]{2,1,0:T(8,128)(2,1)S(1)} %collective-permute-done.10.other_ref), custom_call_target="tpu_custom_call" | custom-call | tf_op jit(solution)/shard_map/wiener/pallas_call | solution.py:629
  96.4 1.3 %collective-permute-start.12 = (bf16[8,64,128]{2,1,0:T(8,128)(2,1)}, bf16[8,64,128]{2,1,0:T(8,128)(2,1)S(1)}, u32[]{:S(2)}, u32[]{:S(2)}) collective-permute-start(bf16[8,64,128]{2,1,0:T(8,128)(2,1)} %wiener.1.refs_4_), channel_id=1, source_target_pairs={{0,16},{8,24},{16,0},{24,8},{1,17},{9,25},{17,1},{25,9},{2,18},{10... | collective-permute-start | bytes 393224 | tf_op jit(solution)/shard_map/ppermute | solution.py:579
  97.6 5.6 %all-to-all-start.1 = ((bf16[8,64,128]{2,1,0:T(8,128)(2,1)}), bf16[8,64,128]{2,1,0:T(8,128)(2,1)S(1)}, u32[]{:S(2)}, u32[]{:S(2)}) async-start(bf16[8,64,128]{2,1,0:T(8,128)(2,1)} %wiener.1.refs_4_), calls=%async_computation.1 | async-start | bytes 262144 | tf_op jit(solution)/shard_map/all_to_all | solution.py:698
  103.2 0.0 collective-permute-start.11
  103.2 0.0 collective-permute-done.12.refs_6_
  103.2 0.5 collective-permute-start.13
  103.7 1.0 collective-permute-done.11.refs_5_
  104.8 0.2 collective-permute-done.13.refs_7_
  104.9 0.6 copy-done.9
  105.6 7.9 %final.1 = bf16[32,64,256]{2,1,0:T(8,128)(2,1)} custom-call(s32[4,8]{1,0:T(4,128)S(1)} %bitcast.24, s32[32]{0:T(128)S(1)} %copy-done.6, s32[1]{0:T(128)} %bitcast.1.here_ref, bf16[32,64,256]{2,1,0:T(8,128)(2,1)} %get-tuple-element.36.third_ref, bf16[8,4,1024,128]{3,2,1,0:T(8,128)(2,1)} %bitcast.31, bf16[8,64,128]{2,1,0:T(8,128)(2,1)S(1)} %all-to-all-done.refs_0_, ...), custom_call_target="tpu_custom_call" | custom-call | tf_op jit(solution)/shard_map/final/pallas_call | solution.py:252
  113.5 0.0 all-to-all-done.1
  113.5 0.8 copy.11
  (18 shorter events, 0.2 us)
Async XLA Ops:
  2.3 14.7 %all-to-all-start = ((bf16[8,64,128]{2,1,0:T(8,128)(2,1)}), bf16[8,64,128]{2,1,0:T(8,128)(2,1)S(1)}, u32[]{:S(2)}, u32[]{:S(2)}) async-start(bf16[8,64,128]{2,1,0:T(8,128)(2,1)} %bitcast.6), calls=%async_computation | async-start | bytes 262144 | tf_op jit(solution)/shard_map/all_to_all | solution.py:660
  9.6 0.7 copy-start.3
  10.3 0.7 copy-start.5
  11.0 7.5 %copy-start.7 = (s32[48,2]{0,1:T(2,128)S(1)}, s32[48,2]{0,1:T(2,128)}, u32[]{:S(2)}) copy-start(s32[48,2]{0,1:T(2,128)} %param.11) | copy-start | bytes 1156
  11.0 12.3 %copy-start.4 = (s32[8,4]{0,1:T(4,128)S(1)}, s32[8,4]{0,1:T(4,128)}, u32[]{:S(2)}) copy-start(s32[8,4]{0,1:T(4,128)} %param.10) | copy-start | bytes 388
  11.0 12.3 %copy-start.6 = (s32[32]{0:T(128)S(1)}, s32[32]{0:T(128)}, u32[]{:S(2)}) copy-start(s32[32]{0:T(128)} %owner_ref.7) | copy-start | bytes 388
  16.9 5.0 %collective-permute-start.1 = (bf16[8,64,128]{2,1,0:T(8,128)(2,1)S(1)}, bf16[8,64,128]{2,1,0:T(8,128)(2,1)S(1)}, u32[]{:S(2)}, u32[]{:S(2)}) collective-permute-start(bf16[8,64,128]{2,1,0:T(8,128)(2,1)S(1)} %all-to-all-done.refs_0_), channel_id=1, source_target_pairs={{0,16},{8,24},{16,0},{24,8},{1,17},{9,25},{17,1},{25,9},{2,18},{10... | collective-permute-start | bytes 393224 | tf_op jit(solution)/shard_map/ppermute | solution.py:579
  18.4 3.6 %collective-permute-start = (bf16[8,64,128]{2,1,0:T(8,128)(2,1)S(1)}, bf16[8,64,128]{2,1,0:T(8,128)(2,1)S(1)}, u32[]{:S(2)}, u32[]{:S(2)}) collective-permute-start(bf16[8,64,128]{2,1,0:T(8,128)(2,1)S(1)} %all-to-all-done.refs_0_), channel_id=1, source_target_pairs={{0,8},{8,0},{16,24},{24,16},{1,9},{9,1},{17,25},{25,17},{2,10},{10... | collective-permute-start | bytes 393224 | tf_op jit(solution)/shard_map/ppermute | solution.py:579
  21.9 1.3 %collective-permute-start.2 = (bf16[8,64,128]{2,1,0:T(8,128)(2,1)S(1)}, bf16[8,64,128]{2,1,0:T(8,128)(2,1)S(1)}, u32[]{:S(2)}, u32[]{:S(2)}) collective-permute-start(bf16[8,64,128]{2,1,0:T(8,128)(2,1)S(1)} %collective-permute-done.1.refs_2_), channel_id=1, source_target_pairs={{0,8},{8,0},{16,24},{24,16},{1,9},{9,1},{17,25},{25,17},{2,10},{10... | collective-permute-start | bytes 393224 | tf_op jit(solution)/shard_map/ppermute | solution.py:579
  23.3 12.4 %copy-start.8 = (f32[48,32,256]{2,1,0:T(8,128)S(1)}, f32[48,32,256]{2,1,0:T(8,128)}, u32[]{:S(2)}) copy-start(f32[48,32,256]{2,1,0:T(8,128)} %param.12) | copy-start | bytes 4718596
  32.0 5.0 %collective-permute-start.3 = (bf16[8,64,256]{2,1,0:T(8,128)(2,1)S(1)}, bf16[8,64,256]{2,1,0:T(8,128)(2,1)S(1)}, u32[]{:S(2)}, u32[]{:S(2)}) collective-permute-start(bf16[8,64,256]{2,1,0:T(8,128)(2,1)S(1)} %get-tuple-element.25), channel_id=1, source_target_pairs={{8,16},{16,8},{9,17},{17,9},{10,18},{18,10},{11,19},{19,11},{12,20... | collective-permute-start | bytes 786440 | tf_op jit(solution)/shard_map/ppermute | solution.py:419
  32.7 4.4 %collective-permute-start.4 = (bf16[8,64,256]{2,1,0:T(8,128)(2,1)}, bf16[8,64,256]{2,1,0:T(8,128)(2,1)S(1)}, u32[]{:S(2)}, u32[]{:S(2)}) collective-permute-start(bf16[8,64,256]{2,1,0:T(8,128)(2,1)} %get-tuple-element.26), channel_id=1, source_target_pairs={{0,8},{16,24},{8,0},{24,16},{1,9},{17,25},{9,1},{25,17},{2,10},{18... | collective-permute-start | bytes 786440 | tf_op jit(solution)/shard_map/ppermute | solution.py:419
  36.0 1.2 %copy-start.2 = (bf16[32,64,256]{2,1,0:T(8,128)(2,1)S(1)}, bf16[32,64,256]{2,1,0:T(8,128)(2,1)}, u32[]{:S(2)}) copy-start(bf16[32,64,256]{2,1,0:T(8,128)(2,1)} %get-tuple-element.30.field_ref) | copy-start | bytes 3145732
  37.1 11.9 %copy-start = (bf16[48,32,8,256]{3,2,1,0:T(8,128)(2,1)}, bf16[48,32,8,256]{3,2,1,0:T(8,128)(2,1)S(1)}, u32[]{:S(2)}) copy-start(bf16[48,32,8,256]{3,2,1,0:T(8,128)(2,1)S(1)} %spread.1.weights_ref) | copy-start | bytes 18874372
  49.0 1.0 copy-start.1
  50.0 6.1 %collective-permute-start.5 = (bf16[8,64,256]{2,1,0:T(8,128)(2,1)S(1)}, bf16[8,64,256]{2,1,0:T(8,128)(2,1)S(1)}, u32[]{:S(2)}, u32[]{:S(2)}) collective-permute-start(bf16[8,64,256]{2,1,0:T(8,128)(2,1)S(1)} %get-tuple-element.32), channel_id=1, source_target_pairs={{8,16},{16,8},{9,17},{17,9},{10,18},{18,10},{11,19},{19,11},{12,20... | collective-permute-start | bytes 786440 | tf_op jit(solution)/shard_map/ppermute | solution.py:419
  50.6 6.6 %collective-permute-start.6 = (bf16[8,64,256]{2,1,0:T(8,128)(2,1)S(1)}, bf16[8,64,256]{2,1,0:T(8,128)(2,1)S(1)}, u32[]{:S(2)}, u32[]{:S(2)}) collective-permute-start(bf16[8,64,256]{2,1,0:T(8,128)(2,1)S(1)} %get-tuple-element.33), channel_id=1, source_target_pairs={{0,8},{16,24},{8,0},{24,16},{1,9},{17,25},{9,1},{25,17},{2,10},{18... | collective-permute-start | bytes 786440 | tf_op jit(solution)/shard_map/ppermute | solution.py:419
  75.8 4.3 %collective-permute-start.7 = (bf16[1056,128]{1,0:T(8,128)(2,1)S(1)}, bf16[1056,128]{1,0:T(8,128)(2,1)S(1)}, u32[]{:S(2)}, u32[]{:S(2)}) collective-permute-start(bf16[1056,128]{1,0:T(8,128)(2,1)S(1)} %get-tuple-element.38), channel_id=1, source_target_pairs={{0,8},{8,0},{16,24},{24,16},{1,9},{9,1},{17,25},{25,17},{2,10},{10... | collective-permute-start | bytes 811016 | tf_op jit(solution)/shard_map/ppermute | solution.py:589
  80.3 10.0 %copy-start.10 = (f32[129]{0:T(256)S(1)}, f32[129]{0:T(256)}, u32[]{:S(2)}) copy-start(f32[129]{0:T(256)} %param.15) | copy-start | bytes 1552
  80.4 5.9 %collective-permute-start.8 = (bf16[528,128]{1,0:T(8,128)(2,1)S(1)}, bf16[528,128]{1,0:T(8,128)(2,1)S(1)}, u32[]{:S(2)}, u32[]{:S(2)}) collective-permute-start(bf16[528,128]{1,0:T(8,128)(2,1)S(1)} %pad_maximum_fusion), channel_id=1, source_target_pairs={{0,16},{8,24},{16,0},{24,8},{1,17},{9,25},{17,1},{25,9},{2,18},{10... | collective-permute-start | bytes 405512 | tf_op jit(solution)/shard_map/ppermute | solution.py:589
  86.5 4.0 %collective-permute-start.10 = (bf16[8,64,128]{2,1,0:T(8,128)(2,1)S(1)}, bf16[8,64,128]{2,1,0:T(8,128)(2,1)S(1)}, u32[]{:S(2)}, u32[]{:S(2)}) collective-permute-start(bf16[8,64,128]{2,1,0:T(8,128)(2,1)S(1)} %get-tuple-element.42), channel_id=1, source_target_pairs={{1,2},{3,4},{5,6},{2,1},{4,3},{6,5},{9,10},{11,12},{13,14},{10,9},... | collective-permute-start | bytes 393224 | tf_op jit(solution)/shard_map/ppermute | solution.py:691
  87.1 7.8 %collective-permute-start.9 = (bf16[8,64,128]{2,1,0:T(8,128)(2,1)S(1)}, bf16[8,64,128]{2,1,0:T(8,128)(2,1)S(1)}, u32[]{:S(2)}, u32[]{:S(2)}) collective-permute-start(bf16[8,64,128]{2,1,0:T(8,128)(2,1)S(1)} %get-tuple-element.42), channel_id=1, source_target_pairs={{0,1},{1,0},{2,3},{3,2},{4,5},{5,4},{6,7},{7,6},{8,9},{9,8},{10,11... | collective-permute-start | bytes 393224 | tf_op jit(solution)/shard_map/ppermute | solution.py:690
  96.4 6.8 %collective-permute-start.12 = (bf16[8,64,128]{2,1,0:T(8,128)(2,1)}, bf16[8,64,128]{2,1,0:T(8,128)(2,1)S(1)}, u32[]{:S(2)}, u32[]{:S(2)}) collective-permute-start(bf16[8,64,128]{2,1,0:T(8,128)(2,1)} %wiener.1.refs_4_), channel_id=1, source_target_pairs={{0,16},{8,24},{16,0},{24,8},{1,17},{9,25},{17,1},{25,9},{2,18},{10... | collective-permute-start | bytes 393224 | tf_op jit(solution)/shard_map/ppermute | solution.py:579
  97.6 15.9 %all-to-all-start.1 = ((bf16[8,64,128]{2,1,0:T(8,128)(2,1)}), bf16[8,64,128]{2,1,0:T(8,128)(2,1)S(1)}, u32[]{:S(2)}, u32[]{:S(2)}) async-start(bf16[8,64,128]{2,1,0:T(8,128)(2,1)} %wiener.1.refs_4_), calls=%async_computation.1 | async-start | bytes 262144 | tf_op jit(solution)/shard_map/all_to_all | solution.py:698
  103.2 1.6 %collective-permute-start.11 = (bf16[8,64,128]{2,1,0:T(8,128)(2,1)}, bf16[8,64,128]{2,1,0:T(8,128)(2,1)S(1)}, u32[]{:S(2)}, u32[]{:S(2)}) collective-permute-start(bf16[8,64,128]{2,1,0:T(8,128)(2,1)} %wiener.1.refs_4_), channel_id=1, source_target_pairs={{0,8},{8,0},{16,24},{24,16},{1,9},{9,1},{17,25},{25,17},{2,10},{10... | collective-permute-start | bytes 393224 | tf_op jit(solution)/shard_map/ppermute | solution.py:579
  103.2 1.7 %collective-permute-start.13 = (bf16[8,64,128]{2,1,0:T(8,128)(2,1)S(1)}, bf16[8,64,128]{2,1,0:T(8,128)(2,1)S(1)}, u32[]{:S(2)}, u32[]{:S(2)}) collective-permute-start(bf16[8,64,128]{2,1,0:T(8,128)(2,1)S(1)} %collective-permute-done.12.refs_6_), channel_id=1, source_target_pairs={{0,8},{8,0},{16,24},{24,16},{1,9},{9,1},{17,25},{25,17},{2,10},{10... | collective-permute-start | bytes 393224 | tf_op jit(solution)/shard_map/ppermute | solution.py:579
  104.9 0.6 copy-start.9
